TPU v7x, 512 devices: a whole 4x8x8 slice. The times are simulated.
512 devices in a mesh: dp: 8 (over z_lo, core), seq: 64 (over x, y, z_hi).
Axes of the slice: x: 4, y: 8, z: 8 (z_hi: 2, z_lo: 4; z = z_hi * 4 + z_lo), core: 2. Of those that a mesh axis runs over, the one named last changes fastest.
Arguments:
- queries: bfloat16 [8, 8192, 1024], P('dp', 'seq'), may hold values from -6 to 6
- keys: bfloat16 [8, 8192, 1024], P('dp', 'seq'), may hold values from -6 to 6
- values: bfloat16 [8, 8192, 1024], P('dp', 'seq'), may hold values from -6 to 6
- grad_out: bfloat16 [8, 8192, 1024], P('dp', 'seq'), may hold values from -6 to 6
- mem_keys: bfloat16 [64, 512, 1024], P('dp', 'seq'), may hold values from -6 to 6
- mem_values: bfloat16 [64, 512, 1024], P('dp', 'seq'), may hold values from -6 to 6
- seq_lengths: int32 [8], replicated, may hold values from 256 to 8192, as said below
- mem_counts: int32 [8], replicated, may hold values from 1 to 4, as said below
- block_lists: int32 [8, 4], replicated, may hold values from 0 to 63, as said below
- block_slots: int32 [64], replicated, may hold values from 0 to 63, each once
Outputs:
- grad_queries: bfloat16 [8, 8192, 1024], P('dp', 'seq')
- grad_keys: bfloat16 [8, 8192, 1024], P('dp', 'seq')
- grad_values: bfloat16 [8, 8192, 1024], P('dp', 'seq')
Inputs may be any that keep to these rules, and one draw needn't show every extreme that they name: `seq_lengths`: some user has all 8192 events. `mem_counts`: some user attends to all 4 listed blocks. `block_lists`: the 4 ids of one user are distinct. `block_slots`: A permutation of the block ids.
All inputs are finite; a program needn't handle non-finite values.
Results may differ from a plain program's by a relative error of at most 0.0063.
Values may be sent and summed in bfloat16 or wider, within the bound.
A program may use at most 128 MiB of HBM per device.

v0:
```python
import math

import jax
import jax.numpy as jnp
from jax import lax
from jax.sharding import PartitionSpec as P

H = 8
WINDOW = 512


def passed_along(value, axis, by):
    count = lax.axis_size(axis)
    pairs = [(i, i + by) for i in range(count) if 0 <= i + by < count]
    return lax.ppermute(value, axis, pairs)


def head_terms(query_h, key_h, value_h, grad_h, memk_h, memv_h, allow_window, allow_memory):
    scaling = 1.0 / math.sqrt(query_h.shape[1])
    score_w = jnp.dot(query_h, key_h.T, preferred_element_type=jnp.float32) * scaling
    score_m = jnp.dot(query_h, memk_h.T, preferred_element_type=jnp.float32) * scaling
    score_w = jnp.where(allow_window, score_w, -1e30)
    score_m = jnp.where(allow_memory, score_m, -1e30)
    row_top = jnp.maximum(jnp.max(score_w, axis=1), jnp.max(score_m, axis=1))
    expo_w = jnp.exp(score_w - row_top[:, None])
    expo_m = jnp.exp(score_m - row_top[:, None])
    totals = jnp.sum(expo_w, axis=1) + jnp.sum(expo_m, axis=1)
    prob_w = expo_w / totals[:, None]
    prob_m = expo_m / totals[:, None]
    half_w = prob_w.astype(jnp.bfloat16)
    half_m = prob_m.astype(jnp.bfloat16)
    output = jnp.dot(half_w, value_h, preferred_element_type=jnp.float32) + jnp.dot(
        half_m, memv_h, preferred_element_type=jnp.float32
    )
    deltas = jnp.sum(grad_h.astype(jnp.float32) * output, axis=1)
    dprob_w = jnp.dot(grad_h, value_h.T, preferred_element_type=jnp.float32)
    dprob_m = jnp.dot(grad_h, memv_h.T, preferred_element_type=jnp.float32)
    dscore_w = (prob_w * (dprob_w - deltas[:, None])).astype(jnp.bfloat16)
    dscore_m = (prob_m * (dprob_m - deltas[:, None])).astype(jnp.bfloat16)
    grad_query = (
        jnp.dot(dscore_w, key_h, preferred_element_type=jnp.float32)
        + jnp.dot(dscore_m, memk_h, preferred_element_type=jnp.float32)
    ) * scaling
    grad_key = jnp.dot(dscore_w.T, query_h, preferred_element_type=jnp.float32) * scaling
    grad_value = jnp.dot(half_w.T, grad_h, preferred_element_type=jnp.float32)
    return (grad_query, grad_key, grad_value, row_top, totals, deltas)


def combine_heads(stacked):
    return jnp.transpose(stacked, (1, 0, 2)).reshape(
        stacked.shape[1], stacked.shape[0] * stacked.shape[2]
    )


def all_heads(
    query_rows, key_rows, value_rows, grad_rows, memk_rows, memv_rows, allow_window, allow_memory
):
    width = query_rows.shape[1] // H

    def per_head(index):

        def column_slice(tensor):
            return lax.dynamic_slice_in_dim(tensor, index * width, width, 1)

        return head_terms(
            column_slice(query_rows),
            column_slice(key_rows),
            column_slice(value_rows),
            column_slice(grad_rows),
            column_slice(memk_rows),
            column_slice(memv_rows),
            allow_window,
            allow_memory,
        )

    grad_query, grad_key, grad_value, row_top, totals, deltas = lax.map(
        per_head, jnp.arange(H, dtype=jnp.int32)
    )
    return (
        combine_heads(grad_query),
        combine_heads(grad_key),
        combine_heads(grad_value),
        jnp.stack([row_top, totals, deltas]),
    )


def on_device(
    queries,
    keys,
    values,
    grad_out,
    mem_keys,
    mem_values,
    seq_lengths,
    mem_counts,
    block_lists,
    block_slots,
):
    rows = queries.shape[1]
    width = queries.shape[2]
    reach = WINDOW // rows
    shard = lax.axis_index("seq")
    owner_me = lax.axis_index("dp")
    length = lax.dynamic_index_in_dim(seq_lengths, owner_me, 0, keepdims=False)
    count = lax.dynamic_index_in_dim(mem_counts, owner_me, 0, keepdims=False)
    own_pair = jnp.stack([keys[0], values[0]])
    earlier = [passed_along(own_pair, "seq", offset) for offset in range(1, reach + 1)]
    window_pair = jnp.concatenate(earlier[::-1] + [own_pair], axis=1)
    pool_pair = jnp.stack([mem_keys, mem_values])
    block_range = jnp.arange(block_slots.shape[0], dtype=jnp.int32)
    slot_table = jnp.sum(
        jnp.where(
            block_range[None, None, :] == block_lists[:, :, None], block_slots[None, None, :], 0
        ),
        axis=2,
    )
    whole_pool = lax.all_gather(pool_pair, "dp", axis=1, tiled=True)
    my_slots = lax.dynamic_index_in_dim(slot_table, owner_me, 0, keepdims=False)
    chosen = jnp.take(whole_pool, my_slots, axis=1)
    memory_pair = lax.all_gather(chosen, "seq", axis=2, tiled=True)
    memory_pair = memory_pair.reshape(2, memory_pair.shape[1] * memory_pair.shape[2], width)
    memory_events = memory_pair.shape[1]
    block_size = memory_events // chosen.shape[1]
    query_pos = shard * rows + jnp.arange(rows, dtype=jnp.int32)
    key_pos = (shard - reach) * rows + jnp.arange((reach + 1) * rows, dtype=jnp.int32)
    allow_window = (
        (key_pos[None, :] <= query_pos[:, None])
        & (query_pos[:, None] - key_pos[None, :] < WINDOW)
        & (key_pos[None, :] >= 0)
        & ((key_pos[None, :] < length) | (key_pos[None, :] == query_pos[:, None]))
    )
    allow_memory = (jnp.arange(memory_events, dtype=jnp.int32) // block_size < count)[None, :]
    masked = grad_out[0] * (query_pos < length)[:, None].astype(jnp.bfloat16)
    grad_query, grad_key, grad_value, row_stats = all_heads(
        queries[0],
        window_pair[0],
        window_pair[1],
        masked,
        memory_pair[0],
        memory_pair[1],
        allow_window,
        allow_memory,
    )
    grad_pair = jnp.stack([grad_key, grad_value])
    totals = grad_pair[:, reach * rows :]
    for back in range(1, reach + 1):
        piece = grad_pair[:, (reach - back) * rows : (reach - back + 1) * rows]
        totals = totals + passed_along(piece, "seq", -back)
    return (
        grad_query.astype(jnp.bfloat16)[None],
        totals[0].astype(jnp.bfloat16)[None],
        totals[1].astype(jnp.bfloat16)[None],
    )


def solution(mesh):
    placed = (
        P("dp", "seq", None),
        P("dp", "seq", None),
        P("dp", "seq", None),
        P("dp", "seq", None),
        P("dp", "seq", None),
        P("dp", "seq", None),
        P(),
        P(),
        P(),
        P(),
    )
    return jax.shard_map(
        on_device,
        mesh=mesh,
        in_specs=placed,
        out_specs=(P("dp", "seq", None), P("dp", "seq", None), P("dp", "seq", None)),
        check_vma=False,
    )
```

profile of v0, /device:TPU:168, one launch (start us, length us, event | category | flops | bytes accessed | tf_op | source)
XLA Modules:
  0.0 655.5 jit_solution(4557520702945406737)
XLA Ops:
  7.2 1.7 pad_maximum_fusion
  10.2 40.3 %all-gather.3.cloned.1.call-done = bf16[2,64,8,1024]{3,2,1,0:T(8,128)(2,1)} async-done(((bf16[2,8,8,1024]{3,2,1,0:T(8,128)(2,1)}), bf16[2,64,8,1024]{3,2,1,0:T(8,128)(2,1)}) %all-gather.3.cloned.1.call-update) | async-done | bytes 2097168 | tf_op jit(solution)/shard_map/all_gather | solution.py:117
  50.5 2.1 gather_fusion
  53.4 1.7 constant_dynamic-update-slice_fusion.1
  55.1 1.7 constant_dynamic-update-slice_fusion
  56.7 5.5 collective-permute-start.3
  62.3 2.5 collective-permute-start.2
  64.8 5.0 collective-permute-start.1
  69.8 4.3 collective-permute-start
  74.1 1.2 dynamic_slice.33
  77.6 46.2 %collective-permute-done = bf16[2,128,1024]{2,1,0:T(8,128)(2,1)S(1)} collective-permute-done((bf16[2,128,1024]{2,1,0:T(8,128)(2,1)}, bf16[2,128,1024]{2,1,0:T(8,128)(2,1)S(1)}, u32[]{:S(2)}, u32[]{:S(2)}) %collective-permute-start) | collective-permute-done | bytes 524320 | tf_op jit(solution)/shard_map/ppermute | solution.py:15
  123.8 5.7 collective-permute-done.1
  129.7 1.3 slice_bitcast_fusion
  131.0 183.7 %all-gather.5.cloned.1.call-done = bf16[2,4,512,1024]{3,2,0,1:T(8,128)(2,1)} async-done(((bf16[2,4,8,1024]{3,2,0,1:T(8,128)(2,1)}), bf16[2,4,512,1024]{3,2,0,1:T(8,128)(2,1)}) %all-gather.5.cloned.1.call-update) | async-done | bytes 8388624 | tf_op jit(solution)/shard_map/all_gather | solution.py:120
  314.8 5.9 fusion.72
  320.7 110.0 %while.15 = (s32[]{:T(128)}, bf16[8,128,128]{2,1,0:T(8,128)(2,1)S(1)}, f32[8,640,128]{2,1,0:T(8,128)}, f32[8,640,128]{2,1,0:T(8,128)}, s32[8]{0:T(128)S(1)}, /*i...) while((s32[]{:T(128)}, ...), condition=%wide.region_7.8_spmd.clone, body=%wide.region_1.7_spmd.clone.sunk | while | flops 399836800 | bytes 10319123 | solution.py:76
  323.7 1.4 fusion.119
  326.9 1.5 fusion.123
  329.8 1.8 fusion.126
  332.7 1.7 fusion.127
  337.5 1.4 fusion.119
  340.7 1.5 fusion.123
  343.6 1.8 fusion.126
  346.5 1.7 fusion.127
  351.2 1.4 fusion.119
  354.5 1.5 fusion.123
  357.4 1.8 fusion.126
  360.2 1.7 fusion.127
  365.0 1.4 fusion.119
  368.2 1.5 fusion.123
  371.1 1.8 fusion.126
  374.0 1.7 fusion.127
  378.7 1.4 fusion.119
  381.9 1.5 fusion.123
  384.8 1.8 fusion.126
  387.7 1.7 fusion.127
  392.5 1.4 fusion.119
  395.7 1.5 fusion.123
  398.6 1.8 fusion.126
  401.4 1.7 fusion.127
  406.2 1.4 fusion.119
  409.4 1.5 fusion.123
  412.3 1.8 fusion.126
  415.2 1.7 fusion.127
  420.0 1.4 fusion.119
  423.2 1.5 fusion.123
  426.1 1.8 fusion.126
  429.0 1.7 fusion.127
  430.7 4.9 copy.25
  435.6 2.6 stack_reshape.7
  438.1 4.8 copy.24
  442.9 3.7 stack_reshape.6
  446.7 1.9 constant_dynamic-update-slice_fusion.9
  448.9 2.0 fusion.73
  450.9 1.6 copy-done
  452.6 5.0 collective-permute-start.4
  457.5 4.0 collective-permute-start.7
  461.5 5.6 collective-permute-start.6
  467.0 2.6 collective-permute-start.5
  470.7 33.2 %collective-permute-done.4 = f32[2,128,1024]{2,1,0:T(8,128)S(1)} collective-permute-done((f32[2,128,1024]{2,1,0:T(8,128)}, f32[2,128,1024]{2,1,0:T(8,128)S(1)}, u32[]{:S(2)}, u32[]{:S(2)}) %collective-permute-start.4) | collective-permute-done | bytes 1048608 | tf_op jit(solution)/shard_map/ppermute | solution.py:15
  503.8 19.7 %collective-permute-done.7 = f32[2,128,1024]{2,1,0:T(8,128)S(1)} collective-permute-done((f32[2,128,1024]{2,1,0:T(8,128)}, f32[2,128,1024]{2,1,0:T(8,128)S(1)}, u32[]{:S(2)}, u32[]{:S(2)}) %collective-permute-start.7) | collective-permute-done | bytes 1048608 | tf_op jit(solution)/shard_map/ppermute | solution.py:15
  523.5 37.4 %collective-permute-done.6 = f32[2,128,1024]{2,1,0:T(8,128)S(1)} collective-permute-done((f32[2,128,1024]{2,1,0:T(8,128)}, f32[2,128,1024]{2,1,0:T(8,128)S(1)}, u32[]{:S(2)}, u32[]{:S(2)}) %collective-permute-start.6) | collective-permute-done | bytes 1048608 | tf_op jit(solution)/shard_map/ppermute | solution.py:15
  560.9 84.9 %collective-permute-done.5 = f32[2,128,1024]{2,1,0:T(8,128)} collective-permute-done((f32[2,128,1024]{2,1,0:T(8,128)}, f32[2,128,1024]{2,1,0:T(8,128)}, u32[]{:S(2)}, u32[]{:S(2)}) %collective-permute-start.5) | collective-permute-done | bytes 1048608 | tf_op jit(solution)/shard_map/ppermute | solution.py:15
  645.8 2.0 fusion.66
  (134 shorter events, 59.0 us)
Async XLA Ops:
  7.2 68.2 %copy-start.3 = (bf16[1,128,1024]{2,1,0:T(8,128)(2,1)S(1)}, bf16[1,128,1024]{2,1,0:T(8,128)(2,1)}, u32[]{:S(2)}) copy-start(bf16[1,128,1024]{2,1,0:T(8,128)(2,1)} %param.15) | copy-start | bytes 786436
  7.2 69.8 %copy-start.6 = (s32[8]{0:T(128)S(1)}, s32[8]{0:T(128)}, u32[]{:S(2)}) copy-start(s32[8]{0:T(128)} %param.19) | copy-start | bytes 100
  7.2 43.3 %all-gather.3.cloned.1.call-start = ((), (), s32[]{:S(2)}) async-start(), calls=%async_computation | async-start | bytes 2359296 | tf_op jit(solution)/shard_map/all_gather | solution.py:117
  9.0 305.8 %all-gather.5.cloned.1.call-start = ((), (), s32[]{:S(2)}) async-start(), calls=%async_computation.1 | async-start | bytes 8519680 | tf_op jit(solution)/shard_map/all_gather | solution.py:120
  56.7 72.8 %collective-permute-start.3 = (bf16[2,128,1024]{2,1,0:T(8,128)(2,1)}, bf16[2,128,1024]{2,1,0:T(8,128)(2,1)S(1)}, u32[]{:S(2)}, u32[]{:S(2)}) collective-permute-start(bf16[2,128,1024]{2,1,0:T(8,128)(2,1)} %constant_dynamic-update-slice_fusion), channel_id=1, source_target_pairs={{0,1},{1,2},{2,3},{3,4},{4,5},{5,6},{6,7},{7,8},{8,9},{9,10},{10,1... | collective-permute-start | bytes 1572872 | tf_op jit(solution)/shard_map/ppermute | solution.py:15
  62.3 67.3 %collective-permute-start.2 = (bf16[2,128,1024]{2,1,0:T(8,128)(2,1)}, bf16[2,128,1024]{2,1,0:T(8,128)(2,1)S(1)}, u32[]{:S(2)}, u32[]{:S(2)}) collective-permute-start(bf16[2,128,1024]{2,1,0:T(8,128)(2,1)} %constant_dynamic-update-slice_fusion), channel_id=1, source_target_pairs={{0,2},{1,3},{2,4},{3,5},{4,6},{5,7},{6,8},{7,9},{8,10},{9,11},{10,... | collective-permute-start | bytes 1572872 | tf_op jit(solution)/shard_map/ppermute | solution.py:15
  64.8 64.7 %collective-permute-start.1 = (bf16[2,128,1024]{2,1,0:T(8,128)(2,1)}, bf16[2,128,1024]{2,1,0:T(8,128)(2,1)S(1)}, u32[]{:S(2)}, u32[]{:S(2)}) collective-permute-start(bf16[2,128,1024]{2,1,0:T(8,128)(2,1)} %constant_dynamic-update-slice_fusion), channel_id=1, source_target_pairs={{0,3},{1,4},{2,5},{3,6},{4,7},{5,8},{6,9},{7,10},{8,11},{9,12},{10... | collective-permute-start | bytes 1572872 | tf_op jit(solution)/shard_map/ppermute | solution.py:15
  69.8 54.0 %collective-permute-start = (bf16[2,128,1024]{2,1,0:T(8,128)(2,1)}, bf16[2,128,1024]{2,1,0:T(8,128)(2,1)S(1)}, u32[]{:S(2)}, u32[]{:S(2)}) collective-permute-start(bf16[2,128,1024]{2,1,0:T(8,128)(2,1)} %constant_dynamic-update-slice_fusion), channel_id=1, source_target_pairs={{0,4},{1,5},{2,6},{3,7},{4,8},{5,9},{6,10},{7,11},{8,12},{9,13},{1... | collective-permute-start | bytes 1572872 | tf_op jit(solution)/shard_map/ppermute | solution.py:15
  75.3 54.3 %copy-start.1 = (bf16[1,128,1024]{2,1,0:T(8,128)(2,1)S(1)}, bf16[1,128,1024]{2,1,0:T(8,128)(2,1)}, u32[]{:S(2)}) copy-start(bf16[1,128,1024]{2,1,0:T(8,128)(2,1)} %param.13) | copy-start | bytes 786436
  76.2 53.5 %copy-start.2 = (bf16[1,128,1024]{2,1,0:T(8,128)(2,1)S(1)}, bf16[1,128,1024]{2,1,0:T(8,128)(2,1)}, u32[]{:S(2)}) copy-start(bf16[1,128,1024]{2,1,0:T(8,128)(2,1)} %param.14) | copy-start | bytes 786436
  430.7 4.9 copy-start.4
  448.9 3.7 copy-start
  448.9 20.7 %copy-start.5 = (bf16[8,128,128]{2,1,0:T(8,128)(2,1)S(1)}, bf16[8,128,128]{2,1,0:T(8,128)(2,1)}, u32[]{:S(2)}) copy-start(bf16[8,128,128]{2,1,0:T(8,128)(2,1)} %copy-done.4) | copy-start | bytes 786436
  452.6 51.3 %collective-permute-start.4 = (f32[2,128,1024]{2,1,0:T(8,128)}, f32[2,128,1024]{2,1,0:T(8,128)S(1)}, u32[]{:S(2)}, u32[]{:S(2)}) collective-permute-start(f32[2,128,1024]{2,1,0:T(8,128)} %get-tuple-element.153), channel_id=1, source_target_pairs={{1,0},{2,1},{3,2},{4,3},{5,4},{6,5},{7,6},{8,7},{9,8},{10,9},{11,1... | collective-permute-start | bytes 3145736 | tf_op jit(solution)/shard_map/ppermute | solution.py:15
  457.5 66.0 %collective-permute-start.7 = (f32[2,128,1024]{2,1,0:T(8,128)}, f32[2,128,1024]{2,1,0:T(8,128)S(1)}, u32[]{:S(2)}, u32[]{:S(2)}) collective-permute-start(f32[2,128,1024]{2,1,0:T(8,128)} %get-tuple-element.154), channel_id=1, source_target_pairs={{4,0},{5,1},{6,2},{7,3},{8,4},{9,5},{10,6},{11,7},{12,8},{13,9},{1... | collective-permute-start | bytes 3145736 | tf_op jit(solution)/shard_map/ppermute | solution.py:15
  461.5 99.5 %collective-permute-start.6 = (f32[2,128,1024]{2,1,0:T(8,128)}, f32[2,128,1024]{2,1,0:T(8,128)S(1)}, u32[]{:S(2)}, u32[]{:S(2)}) collective-permute-start(f32[2,128,1024]{2,1,0:T(8,128)} %get-tuple-element.155), channel_id=1, source_target_pairs={{3,0},{4,1},{5,2},{6,3},{7,4},{8,5},{9,6},{10,7},{11,8},{12,9},{13... | collective-permute-start | bytes 3145736 | tf_op jit(solution)/shard_map/ppermute | solution.py:15
  467.0 178.8 %collective-permute-start.5 = (f32[2,128,1024]{2,1,0:T(8,128)}, f32[2,128,1024]{2,1,0:T(8,128)}, u32[]{:S(2)}, u32[]{:S(2)}) collective-permute-start(f32[2,128,1024]{2,1,0:T(8,128)} %get-tuple-element.156), channel_id=1, source_target_pairs={{2,0},{3,1},{4,2},{5,3},{6,4},{7,5},{8,6},{9,7},{10,8},{11,9},{12,... | collective-permute-start | bytes 3145736 | tf_op jit(solution)/shard_map/ppermute | solution.py:15
Sparse Core Ops, SparseCore 0:
  10.7 39.7 all-gather.2
  55.6 259.1 all-gather.4
where the time goes:
time: 659 us; the launch traced here: 655 us
  waiting for transfers between devices  451 us (68%)
  matrix products  90.2 us (14%)
  local copies, waits for them, and re-layouts  43.4 us (7%)
  starting transfers between devices  34.5 us (5%)
  other arithmetic  16.4 us (2%)
  between operations  14.4 us (2%)
    ppermute x8, waiting for transfers between devices, passed_along(): return lax.ppermute(value, axis, pairs)  227 us
    all_gather x1, waiting for transfers between devices, on_device(): memory_pair = lax.all_gather(chosen, 'seq', axis=2, tiled=True)  184 us
    all_gather x1, waiting for transfers between devices, on_device(): whole_pool = lax.all_gather(pool_pair, 'dp', axis=1, tiled=True)  40.3 us
    ppermute x8, starting transfers between devices, passed_along(): return lax.ppermute(value, axis, pairs)  34.4 us
    dot_general x8, matrix products, head_terms(): jnp.dot(dscore_m, memk_h, preferred_element_type=jnp.float32)  14.3 us
    dot_general x8, matrix products, head_terms(): jnp.dot(dscore_w.T, query_h, preferred_element_type=jnp.float32) * scaling  13.8 us
  transfers between devices with their start and end apart: 10, of which 8 were waited for; matrix products, arithmetic and copies ran while one was open for 2% of the time, Pallas kernels for 0%

commit v1 on v0

v1 whole, which is shorter than its diff:
```python
import functools
import math

import jax
import jax.numpy as jnp
from jax import lax
from jax.experimental import pallas as pl
from jax.experimental.pallas import tpu as pltpu
from jax.sharding import PartitionSpec as P

MESH = pl.DeviceIdType.MESH
ANY = pl.BlockSpec(memory_space=pl.ANY)
VMEM = pl.BlockSpec(memory_space=pltpu.VMEM)
SMEM = pl.BlockSpec(memory_space=pltpu.SMEM)
H = 8
WINDOW = 512
BLK = 512
NX, NY, NZ, ZL = 4, 8, 2, 4
ROWS, HEAD = 128, 128
PAIR = NZ * ROWS
GROUP = [(a, b) for a in range(NX) for b in range(NZ)]
LOG2E = math.log2(math.e)
BARRED = -1e30


def place():
    dp, seq = lax.axis_index("dp"), lax.axis_index("seq")
    return dp // 2, dp % 2, seq // (NY * NZ), (seq // NZ) % NY, seq % NZ


def device(zl, core, x, y, zh):
    return (zl * 2 + core, (x * NY + y) * NZ + zh)


def greet(partners):
    barrier = pltpu.get_barrier_semaphore()
    for partner in partners:
        pl.semaphore_signal(barrier, inc=1, device_id=partner, device_id_type=MESH)
    pl.semaphore_wait(barrier, len(partners))


def remote(src, dst, send, recv, to):
    return pltpu.make_async_remote_copy(
        src_ref=src, dst_ref=dst, send_sem=send, recv_sem=recv, device_id=to, device_id_type=MESH
    )


def columns(head):
    return pl.ds(pl.multiple_of(head * HEAD, HEAD), HEAD)


def gather_kernel(
    slots, q_ref, g_ref, k_ref, v_ref, poolk_ref, poolv_ref,
    kv_ref, qg_ref, mem_ref,
    staged, from_core, staged_z, from_z, picked,
    own_sem, a2a_send, a2a_recv, core_sems, z_send, z_recv, m_send, m_recv, hop_send, hop_recv, ring_send, ring_recv,
):
    zl, core, x, y, zh = place()
    head = x * NZ + zh
    up, down = (y + 1) % NY, (y + NY - 1) % NY
    above, below = device(zl, core, x, up, zh), device(zl, core, x, down, zh)
    peers = [device(zl, core, (x + a) % NX, y, (zh + b) % NZ) for a, b in GROUP]
    twin = device(zl, 1 - core, x, y, zh)
    line = [device((zl + a) % ZL, core, x, y, zh) for a in range(ZL)]
    greet(peers[1:] + [above, below, twin] + line[1:])

    def shuffle(base, sources, into):
        out = []
        for i, (a, b) in enumerate(GROUP):
            part = columns(((x + a) % NX) * NZ + (zh + b) % NZ)
            for n, source in enumerate(sources):
                src, dst = source.at[0, :, part], into.at[0, x, n, zh]
                if i == 0:
                    copy = pltpu.make_async_copy(src, dst, own_sem.at[base + n])
                else:
                    at = (base + n, i)
                    copy = remote(src, dst, a2a_send.at[at], a2a_recv.at[at], peers[i])
                copy.start()
                out.append(copy)
        return out

    kv_moves = shuffle(0, (k_ref, v_ref), kv_ref)

    for z in range(ZL):
        for m in range(4):
            row = slots[(z * 2 + (1 - core)) * 4 + m] % 8
            staged[z, 0, m] = poolk_ref[row]
            staged[z, 1, m] = poolv_ref[row]
    to_twin = remote(staged, from_core, core_sems.at[0], core_sems.at[1], twin)
    to_twin.start()

    qg_moves = shuffle(2, (q_ref, g_ref), qg_ref)

    to_twin.wait()
    for z in range(ZL):
        for m in range(4):
            slot = slots[(z * 2 + core) * 4 + m]
            mine = (slot // 8) % 2 == core
            staged_z[z, 0, m] = jnp.where(mine, poolk_ref[slot % 8], from_core[z, 0, m])
            staged_z[z, 1, m] = jnp.where(mine, poolv_ref[slot % 8], from_core[z, 1, m])
    z_moves = []
    for a in range(1, ZL):
        z_moves.append(
            remote(staged_z.at[(zl + a) % ZL], from_z.at[zl], z_send.at[a], z_recv.at[a], line[a])
        )
        z_moves[-1].start()
    from_z[zl] = staged_z[zl]

    def wait_arrival(copy, i):
        if i == 0:
            copy.wait()
        else:
            copy.wait_recv()

    def first_hop(moves, buf, lane, to, shift):
        out = []
        for a in range(NX):
            for i, (pa, pb) in enumerate(GROUP):
                if pa == a:
                    wait_arrival(moves[2 * i], i)
                    wait_arrival(moves[2 * i + 1], i)
            source = (x + NX - a) % NX
            sems = hop_send.at[lane, 0, a], hop_recv.at[lane, 0, a]
            out.append(remote(buf.at[0, source], buf.at[1, (source + shift) % NX], *sems, to))
            out[-1].start()
        return out

    def second_hop(moves, buf, lane, to, arrived, shift):
        out = []
        for a in range(NX):
            moves[a].wait_recv()
            source = (x + NX - a + arrived) % NX
            sems = hop_send.at[lane, 1, a], hop_recv.at[lane, 1, a]
            out.append(remote(buf.at[1, source], buf.at[2, (source + shift) % NX], *sems, to))
            out[-1].start()
        return out

    top, bottom = (y == NY - 1).astype(jnp.int32), (y == 0).astype(jnp.int32)
    kv_hops = first_hop(kv_moves, kv_ref, 0, above, top)
    qg_hops = first_hop(qg_moves, qg_ref, 1, below, (NX - 1) * bottom)
    kv_hops2 = second_hop(kv_hops, kv_ref, 0, above, bottom, top)

    for move in z_moves:
        move.wait_recv()
    for m in range(4):
        owner = slots[((zl * 2 + core) * 4) + m] // 16
        picked[0, m] = from_z[owner, 0, m]
        picked[1, m] = from_z[owner, 1, m]
    m_moves = []
    for i, (a, b) in enumerate(GROUP):
        part = columns(((x + a) % NX) * NZ + (zh + b) % NZ)
        src, dst = picked.at[:, :, :, part], mem_ref.at[y, :, :, head]
        if i == 0:
            copy = pltpu.make_async_copy(src, dst, own_sem.at[4])
        else:
            copy = remote(src, dst, m_send.at[i], m_recv.at[i], peers[i])
        copy.start()
        m_moves.append(copy)

    qg_hops2 = second_hop(qg_hops, qg_ref, 1, below, (NX - 1) * top, (NX - 1) * bottom)

    for i, copy in enumerate(m_moves):
        wait_arrival(copy, i)
    rising, falling = [], []
    for step in range(NY // 2):
        if step:
            rising[-1].wait_recv()
        piece = mem_ref.at[(y + NY - step) % NY]
        rising.append(remote(piece, piece, ring_send.at[0, step], ring_recv.at[0, step], above))
        rising[-1].start()
        if step < NY // 2 - 1:
            if step:
                falling[-1].wait_recv()
            piece = mem_ref.at[(y + step) % NY]
            falling.append(remote(piece, piece, ring_send.at[1, step], ring_recv.at[1, step], below))
            falling[-1].start()
    rising[-1].wait_recv()
    falling[-1].wait_recv()
    for copy in kv_hops2 + qg_hops2:
        copy.wait()
    for copy in kv_moves[2:] + qg_moves[2:] + z_moves + kv_hops + qg_hops + m_moves[1:] + rising + falling:
        copy.wait_send()


def gather(slots, queries, grads, keys, values, poolk, poolv):
    bf16 = jnp.bfloat16
    window = jax.ShapeDtypeStruct((3, NX, 2, NZ, ROWS, HEAD), bf16)
    dma = pltpu.SemaphoreType.DMA
    return pl.pallas_call(
        gather_kernel,
        name="gather",
        out_shape=(window, window, jax.ShapeDtypeStruct((NY, 2, 4, H, 8, HEAD), bf16)),
        in_specs=[SMEM, ANY, ANY, ANY, ANY, VMEM, VMEM],
        out_specs=(ANY, ANY, ANY),
        scratch_shapes=[
            pltpu.VMEM((ZL, 2, 4, 8, H * HEAD), bf16),
            pltpu.VMEM((ZL, 2, 4, 8, H * HEAD), bf16),
            pltpu.VMEM((ZL, 2, 4, 8, H * HEAD), bf16),
            pltpu.VMEM((ZL, 2, 4, 8, H * HEAD), bf16),
            pltpu.VMEM((2, 4, 8, H * HEAD), bf16),
            dma((5,)),
            dma((4, 8)),
            dma((4, 8)),
            dma((2,)),
            dma((ZL,)),
            dma((ZL,)),
            dma((8,)),
            dma((8,)),
            dma((2, 2, NX)),
            dma((2, 2, NX)),
            dma((2, 4)),
            dma((2, 4)),
        ],
        compiler_params=pltpu.CompilerParams(
            collective_id=0, has_side_effects=True, vmem_limit_bytes=24 << 20
        ),
    )(slots, queries, grads, keys, values, poolk, poolv)


SCALE = LOG2E / math.sqrt(HEAD)
NT = (((1,), (1,)), ((), ()))


def dot_nt(a, b):
    return lax.dot_general(a, b, NT, preferred_element_type=jnp.float32)


def dot(a, b):
    return jnp.dot(a, b, preferred_element_type=jnp.float32)


def halves(op, tile):
    return op(tile[:, :HEAD], tile[:, HEAD:])


def attend_kernel(info, q_ref, kv0_ref, kv1_ref, kv2_ref, mem_ref, gq_ref, stat_ref, scores):
    chunk = pl.program_id(0)
    y, length, count = info[0], info[1], info[2]
    base = (chunk * NY + y) * PAIR
    q = q_ref[0, 0, 0]
    row = lax.broadcasted_iota(jnp.int32, (PAIR, PAIR), 0)
    col = lax.broadcasted_iota(jnp.int32, (PAIR, PAIR), 1)
    pos = lax.broadcasted_iota(jnp.int32, (PAIR, HEAD), 0) + base
    g = jnp.where(pos < length, q_ref[0, 0, 1], jnp.zeros((), jnp.bfloat16))
    kv = (kv0_ref, kv1_ref, kv2_ref)
    tiles = 3 + NY

    def key_value(t):
        if t < 3:
            return kv[t][0, 0, 0], kv[t][0, 0, 1]
        return mem_ref[t - 3, 0], mem_ref[t - 3, 1]

    top = None
    for t in range(tiles):
        s = dot_nt(q, key_value(t)[0]) * SCALE
        if t == 0:
            s = jnp.where((col < row) & (base + col < length) | (col == row), s, BARRED)
        elif t == 1:
            s = jnp.where((base >= PAIR) & (base - PAIR + col < length), s, BARRED)
        elif t == 2:
            s = jnp.where((base >= 2 * PAIR) & (base - 2 * PAIR + col < length) & (row < col), s, BARRED)
        else:
            s = jnp.where(col // (PAIR // 4) < count, s, BARRED)
        scores[t] = s
        part = halves(jnp.maximum, s)
        top = part if top is None else jnp.maximum(top, part)
    top = jnp.max(top, axis=1, keepdims=True)
    total = None
    for t in range(tiles):
        e = jnp.exp2(scores[t] - top)
        scores[t] = e
        part = halves(jnp.add, e)
        total = part if total is None else total + part
    total = jnp.sum(total, axis=1, keepdims=True)
    inverse = 1.0 / total
    output = jnp.zeros((PAIR, HEAD), jnp.float32)
    for t in range(tiles):
        prob = scores[t] * inverse
        scores[t] = prob
        output += dot(prob.astype(jnp.bfloat16), key_value(t)[1])
    delta = jnp.sum(g.astype(jnp.float32) * output, axis=1, keepdims=True)
    grad = jnp.zeros((PAIR, HEAD), jnp.float32)
    for t in range(tiles):
        key, value = key_value(t)
        ds = scores[t] * (dot_nt(g, value) - delta)
        grad += dot(ds.astype(jnp.bfloat16), key)
    gq_ref[0] = (grad * (1.0 / math.sqrt(HEAD))).astype(jnp.bfloat16)
    lse = top + jnp.log(total) * LOG2E
    lane = lax.broadcasted_iota(jnp.int32, (PAIR, HEAD), 1)
    both = jnp.where(lane == 0, lse, delta)
    stat_ref[0] = both.T[:8]


def attend(info, qg, kv, mem):
    chunk = (1, 1, 2, PAIR, HEAD)
    return pl.pallas_call(
        attend_kernel,
        name="attend",
        grid_spec=pltpu.PrefetchScalarGridSpec(
            num_scalar_prefetch=1,
            grid=(NX,),
            in_specs=[
                pl.BlockSpec(chunk, lambda i, _: (0, i, 0, 0, 0)),
                pl.BlockSpec(chunk, lambda i, _: (0, i, 0, 0, 0)),
                pl.BlockSpec(chunk, lambda i, _: (1, i, 0, 0, 0)),
                pl.BlockSpec(chunk, lambda i, _: (2, i, 0, 0, 0)),
                pl.BlockSpec((NY, 2, PAIR, HEAD), lambda i, _: (0, 0, 0, 0)),
            ],
            out_specs=[
                pl.BlockSpec((1, PAIR, HEAD), lambda i, _: (i, 0, 0)),
                pl.BlockSpec((1, 8, PAIR), lambda i, _: (i, 0, 0)),
            ],
            scratch_shapes=[pltpu.VMEM((3 + NY, PAIR, PAIR), jnp.float32)],
        ),
        out_shape=(
            jax.ShapeDtypeStruct((NX, PAIR, HEAD), jnp.bfloat16),
            jax.ShapeDtypeStruct((NX, 8, PAIR), jnp.float32),
        ),
        compiler_params=pltpu.CompilerParams(vmem_limit_bytes=40 << 20),
    )(info, qg, kv, kv, kv, mem)


def stats_kernel(stat_ref, out_ref, own_sem, send, recv):
    zl, core, x, y, zh = place()
    backward = [device(zl, core, x, (y + NY - d) % NY, zh) for d in (1, 2)]
    forward = [device(zl, core, x, (y + d) % NY, zh) for d in (1, 2)]
    barrier = pltpu.get_barrier_semaphore()
    for partner in backward + forward:
        pl.semaphore_signal(barrier, inc=1, device_id=partner, device_id_type=MESH)
    pl.semaphore_wait(barrier, 4)
    own = pltpu.make_async_copy(stat_ref, out_ref.at[0], own_sem)
    own.start()
    copies = []
    for d in (1, 2):
        shift = (NX - 1) * (y < d).astype(jnp.int32)
        for c in range(NX):
            copies.append(
                remote(
                    stat_ref.at[c],
                    out_ref.at[d, (c + shift) % NX],
                    send.at[d - 1, c],
                    recv.at[d - 1, c],
                    backward[d - 1],
                )
            )
            copies[-1].start()
    own.wait()
    for copy in copies:
        copy.wait()


def share_stats(stats):
    return pl.pallas_call(
        stats_kernel,
        name="stats",
        out_shape=jax.ShapeDtypeStruct((3, *stats.shape), stats.dtype),
        in_specs=[ANY],
        out_specs=ANY,
        scratch_shapes=[
            pltpu.SemaphoreType.DMA(()),
            pltpu.SemaphoreType.DMA((2, NX)),
            pltpu.SemaphoreType.DMA((2, NX)),
        ],
        compiler_params=pltpu.CompilerParams(collective_id=1, has_side_effects=True),
    )(stats)


def owe_kernel(info, kv_ref, qg_ref, stat_ref, gk_ref, gv_ref):
    chunk = pl.program_id(0)
    y, length = info[0], info[1]
    base = (chunk * NY + y) * PAIR
    key, value = kv_ref[0, 0, 0], kv_ref[0, 0, 1]
    row = lax.broadcasted_iota(jnp.int32, (PAIR, PAIR), 0)
    col = lax.broadcasted_iota(jnp.int32, (PAIR, PAIR), 1)
    pos = lax.broadcasted_iota(jnp.int32, (PAIR, HEAD), 0) + base
    gk = jnp.zeros((PAIR, HEAD), jnp.float32)
    gv = jnp.zeros((PAIR, HEAD), jnp.float32)
    live = base + row < length
    for d in range(3):
        q = qg_ref[d, 0, 0]
        g = jnp.where(pos + d * PAIR < length, qg_ref[d, 0, 1], jnp.zeros((), jnp.bfloat16))
        lse, delta = stat_ref[d, 0, 0:1], stat_ref[d, 0, 1:2]
        s = dot_nt(key, q) * SCALE - lse
        if d == 0:
            allowed = (row < col) & live | (row == col)
        elif d == 1:
            allowed = live & (base + PAIR < NX * NY * PAIR)
        else:
            allowed = live & (base + 2 * PAIR < NX * NY * PAIR) & (col < row)
        prob = jnp.where(allowed, jnp.exp2(jnp.where(allowed, s, BARRED)), 0.0)
        gv += dot(prob.astype(jnp.bfloat16), g)
        ds = prob * (dot_nt(value, g) - delta)
        gk += dot(ds.astype(jnp.bfloat16), q)
    gk_ref[0] = (gk * (1.0 / math.sqrt(HEAD))).astype(jnp.bfloat16)
    gv_ref[0] = gv.astype(jnp.bfloat16)


def owe(info, kv, qg, stats):
    out = jax.ShapeDtypeStruct((NX, PAIR, HEAD), jnp.bfloat16)
    return pl.pallas_call(
        owe_kernel,
        name="owe",
        grid_spec=pltpu.PrefetchScalarGridSpec(
            num_scalar_prefetch=1,
            grid=(NX,),
            in_specs=[
                pl.BlockSpec((1, 1, 2, PAIR, HEAD), lambda i, _: (0, i, 0, 0, 0)),
                pl.BlockSpec((3, 1, 2, PAIR, HEAD), lambda i, _: (0, i, 0, 0, 0)),
                pl.BlockSpec((3, 1, 8, PAIR), lambda i, _: (0, i, 0, 0)),
            ],
            out_specs=[pl.BlockSpec((1, PAIR, HEAD), lambda i, _: (i, 0, 0))] * 2,
        ),
        out_shape=(out, out),
        compiler_params=pltpu.CompilerParams(vmem_limit_bytes=24 << 20),
    )(info, kv, qg, stats)


def scatter_kernel(*refs):
    sources, outs = refs[:3], refs[3:6]
    own_sem, send, recv = refs[6:]
    zl, core, x, y, zh = place()
    peers = [device(zl, core, (x + a) % NX, y, (zh + b) % NZ) for a, b in GROUP]
    greet(peers[1:])
    part = columns(x * NZ + zh)
    local, copies = [], []
    for i, (a, b) in enumerate(GROUP):
        for n in range(3):
            src, dst = sources[n].at[(x + a) % NX, (zh + b) % NZ], outs[n].at[0, :, part]
            if i == 0:
                local.append(pltpu.make_async_copy(src, dst, own_sem.at[n]))
                local[-1].start()
            else:
                copies.append(remote(src, dst, send.at[n, i], recv.at[n, i], peers[i]))
                copies[-1].start()
    for copy in local + copies:
        copy.wait()


def scatter(*parts):
    out = jax.ShapeDtypeStruct((1, ROWS, H * HEAD), jnp.bfloat16)
    return pl.pallas_call(
        scatter_kernel,
        name="scatter",
        out_shape=(out,) * 3,
        in_specs=[ANY] * 3,
        out_specs=(ANY,) * 3,
        scratch_shapes=[
            pltpu.SemaphoreType.DMA((3,)),
            pltpu.SemaphoreType.DMA((3, 8)),
            pltpu.SemaphoreType.DMA((3, 8)),
        ],
        compiler_params=pltpu.CompilerParams(collective_id=2, has_side_effects=True),
    )(*parts)


def on_device(queries, keys, values, grad_out, mem_keys, mem_values, seq_lengths, mem_counts, block_lists, block_slots):
    user = lax.axis_index("dp")
    y = (lax.axis_index("seq") // NZ) % NY
    ids = jnp.arange(block_slots.shape[0], dtype=jnp.int32)
    slots = jnp.sum(
        jnp.where(ids[None, :] == block_lists.reshape(-1)[:, None], block_slots[None, :], 0), axis=1
    )
    mine = jnp.arange(seq_lengths.shape[0]) == user
    info = jnp.stack(
        [y, jnp.sum(jnp.where(mine, seq_lengths, 0)), jnp.sum(jnp.where(mine, mem_counts, 0))]
    ).astype(jnp.int32)
    kv, qg, mem = gather(slots, queries, grad_out, keys, values, mem_keys, mem_values)
    kv = kv.reshape(3, NX, 2, PAIR, HEAD)
    qg = qg.reshape(3, NX, 2, PAIR, HEAD)
    mem = mem.reshape(NY, 2, PAIR, HEAD)
    gq, stats = attend(info, qg, kv, mem)
    gk, gv = owe(info, kv, qg, share_stats(stats))
    split = (NX, NZ, ROWS, HEAD)
    return scatter(gq.reshape(split), gk.reshape(split), gv.reshape(split))


def solution(mesh):
    rows = P("dp", "seq", None)
    return jax.shard_map(
        on_device,
        mesh=mesh,
        in_specs=(rows,) * 6 + (P(),) * 4,
        out_specs=(rows,) * 3,
        check_vma=False,
    )
```

time: 659 us -> 141 us (0.21)
  the two profiles are of different devices: /device:TPU:168 before, /device:TPU:6 now
where the time goes in v1:
time: 141 us; the launch traced here: 140 us
  Pallas kernels  121 us (86%)
  local copies, waits for them, and re-layouts  15 us (11%)
  other arithmetic  3.52 us (2%)
    pallas_call x1, Pallas kernels, gather(): pl.pallas_call(gather_kernel, name='gather', out_shape=(window, window, j...  73.2 us
    pallas_call x1, Pallas kernels, scatter(): pl.pallas_call(scatter_kernel, name='scatter', out_shape=(out,) * 3, in_s...  24.5 us
    unnamed x26, local copies, waits for them, and re-layouts  15 us
    pallas_call x1, Pallas kernels, attend(): pl.pallas_call(attend_kernel, name='attend', grid_spec=pltpu.PrefetchScal...  10.8 us
    pallas_call x1, Pallas kernels, share_stats(): pl.pallas_call(stats_kernel, name='stats', out_shape=jax.ShapeDtypeStruct...  8.25 us
    pallas_call x1, Pallas kernels, owe(): pl.pallas_call(owe_kernel, name='owe', grid_spec=pltpu.PrefetchScalarGrid...  4.3 us

profile of v1, /device:TPU:6, one launch (start us, length us, event | category | flops | bytes accessed | tf_op | source)
XLA Modules:
  0.0 140.3 jit_solution(18201554759219579707)
XLA Ops:
  0.7 1.3 fusion
  2.0 1.4 pad_add_fusion.info
  3.3 0.8 copy.15
  4.1 0.1 eq.26
  4.2 0.8 select_reduce_fusion.slots
  5.0 0.0 copy-start.1
  5.0 0.9 copy-done.1
  6.0 0.0 copy-start.2
  6.0 0.9 copy-done.2
  6.9 0.0 copy-start.3
  6.9 0.9 copy-done.3
  7.9 0.0 copy-start.4
  7.9 0.9 copy-done.4
  8.8 0.0 copy-start.8
  8.8 0.9 copy-done.8
  9.7 0.0 copy-start.9
  9.7 0.9 copy-done.9
  10.6 73.2 %gather.1 = (bf16[3,4,2,2,128,128]{5,4,3,2,1,0:T(8,128)(2,1)S(1)}, bf16[3,4,2,2,128,128]{5,4,3,2,1,0:T(8,128)(2,1)S(1)}, bf16[8,2,4,8,8,128]{5,4,3,2,1,0:T(8,128)(2,1)S(1)}) custom-call(s32[32]{0:T(128)S(1)} %select_reduce_fusion.slots, bf16[1,128,1024]{2,1,0:T(8,128)(2,1)S(1)} %copy-done.1, bf16[1,128,1024]{2,1,0:T(8,128)(2,1)S(1)} %copy-done.2, ...), custom_call_target="tpu_custom_call" | custom-call | tf_op jit(solution)/shard_map/gather/pallas_call | solution.py:189
  83.8 10.8 %attend.1 = (bf16[4,256,128]{2,1,0:T(8,128)(2,1)S(1)}, f32[4,8,256]{2,1,0:T(8,128)S(1)}) custom-call(s32[3]{0:T(128)S(1)} %pad_add_fusion.info, bf16[3,4,2,256,128]{4,3,2,1,0:T(8,128)(2,1)S(1)} %bitcast.13, bf16[3,4,2,256,128]{4,3,2,1,0:T(8,128)(2,1)S(1)} %bitcast.9, bf16[3,4,2,256,128]{4,3,2,1,0:T(8,128)(2,1)S(1)} %bitcast.10, ...), custom_call_target="tpu_custom_call" | custom-call | tf_op jit(solution)/shard_map/attend/pallas_call | solution.py:296
  94.7 0.0 copy-start.5
  94.7 0.7 copy-done.5
  95.4 0.0 copy-start.10
  95.4 0.6 copy-done.10
  96.0 8.2 %stats.1.stat_ref = f32[3,4,8,256]{3,2,1,0:T(8,128)} custom-call(f32[4,8,256]{2,1,0:T(8,128)} %copy-done.10), custom_call_target="tpu_custom_call" | custom-call | tf_op jit(solution)/shard_map/stats/pallas_call | solution.py:353
  104.2 0.0 copy-start
  104.3 0.9 copy-done
  105.1 4.3 %owe.1 = (bf16[4,256,128]{2,1,0:T(8,128)(2,1)S(1)}, bf16[4,256,128]{2,1,0:T(8,128)(2,1)S(1)}) custom-call(s32[3]{0:T(128)S(1)} %pad_add_fusion.info, bf16[3,4,2,256,128]{4,3,2,1,0:T(8,128)(2,1)S(1)} %bitcast.12, bf16[3,4,2,256,128]{4,3,2,1,0:T(8,128)(2,1)S(1)} %bitcast.14, f32[3,4,8,256]{3,2,1,0:T(8,128)S(1)} %copy-done), custom_call_target="tpu_custom_call" | custom-call | tf_op jit(solution)/shard_map/owe/pallas_call | solution.py:400
  109.4 0.0 copy-start.6
  109.5 0.7 copy-done.6
  110.2 0.0 copy-start.7
  110.2 0.7 copy-done.7
  110.9 24.5 %scatter.1 = (bf16[1,128,1024]{2,1,0:T(8,128)(2,1)}, bf16[1,128,1024]{2,1,0:T(8,128)(2,1)}, bf16[1,128,1024]{2,1,0:T(8,128)(2,1)}) custom-call(bf16[4,2,128,128]{3,2,1,0:T(8,128)(2,1)} %bitcast.16, bf16[4,2,128,128]{3,2,1,0:T(8,128)(2,1)} %bitcast.17, bf16[4,2,128,128]{3,2,1,0:T(8,128)(2,1)} %bitcast.18), custom_call_target="tpu_custom_call" | custom-call | tf_op jit(solution)/shard_map/scatter/pallas_call | solution.py:441
  135.3 1.7 %copy.19 = bf16[1,128,1024]{2,1,0:T(8,128)(2,1)} copy(bf16[1,128,1024]{2,1,0:T(8,128)(2,1)} %get-tuple-element.22) | data formatting | bytes 524288
  137.0 1.7 %copy.20 = bf16[1,128,1024]{2,1,0:T(8,128)(2,1)} copy(bf16[1,128,1024]{2,1,0:T(8,128)(2,1)} %get-tuple-element.23) | data formatting | bytes 524288
  138.7 1.7 %copy.21 = bf16[1,128,1024]{2,1,0:T(8,128)(2,1)} copy(bf16[1,128,1024]{2,1,0:T(8,128)(2,1)} %get-tuple-element.24) | data formatting | bytes 524288
Async XLA Ops:
  5.0 1.0 copy-start.1
  6.0 0.9 copy-start.2
  6.9 0.9 copy-start.3
  7.9 0.9 copy-start.4
  8.8 0.9 copy-start.8
  9.7 0.9 copy-start.9
  94.7 0.7 copy-start.5
  95.4 0.6 copy-start.10
  104.2 0.9 copy-start
  109.4 0.7 copy-start.6
  110.2 0.7 copy-start.7

commit v2 on v0

v2 whole, which is shorter than its diff:
```python
import functools
import math

import jax
import jax.numpy as jnp
from jax import lax
from jax.experimental import pallas as pl
from jax.experimental.pallas import tpu as pltpu
from jax.sharding import PartitionSpec as P

MESH = pl.DeviceIdType.MESH
ANY = pl.BlockSpec(memory_space=pl.ANY)
HBM = pl.BlockSpec(memory_space=pltpu.HBM)
SMEM = pl.BlockSpec(memory_space=pltpu.SMEM)
H = 8
WINDOW = 512
BLK = 512
NX, NY, NZ, ZL = 4, 8, 2, 4
ROWS, HEAD = 128, 128
PAIR = NZ * ROWS
GROUP = [(a, b) for a in range(NX) for b in range(NZ)]
LOG2E = math.log2(math.e)
BARRED = -1e30


def place():
    dp, seq = lax.axis_index("dp"), lax.axis_index("seq")
    return dp // 2, dp % 2, seq // (NY * NZ), (seq // NZ) % NY, seq % NZ


def device(zl, core, x, y, zh):
    return (zl * 2 + core, (x * NY + y) * NZ + zh)


def greet(partners):
    barrier = pltpu.get_barrier_semaphore()
    for partner in partners:
        pl.semaphore_signal(barrier, inc=1, device_id=partner, device_id_type=MESH)
    pl.semaphore_wait(barrier, len(partners))


def remote(src, dst, send, recv, to):
    return pltpu.make_async_remote_copy(
        src_ref=src, dst_ref=dst, send_sem=send, recv_sem=recv, device_id=to, device_id_type=MESH
    )


def columns(head):
    return pl.ds(pl.multiple_of(head * HEAD, HEAD), HEAD)

SCALE = LOG2E / math.sqrt(HEAD)
NT = (((1,), (1,)), ((), ()))


def dot_nt(a, b):
    return lax.dot_general(a, b, NT, preferred_element_type=jnp.float32)


def dot(a, b):
    return jnp.dot(a, b, preferred_element_type=jnp.float32)


def halves(op, tile):
    return op(tile[:, :HEAD], tile[:, HEAD:])


def grid_of(rows, cols):
    return tuple(lax.broadcasted_iota(jnp.int32, (rows, cols), i) for i in range(2))


def attend(base, length, count, q, g, kv_ref, chunk, mem_ref, scores):
    row, col = grid_of(PAIR, PAIR)
    tiles = 3 + NY

    def key_value(t):
        if t < 3:
            return kv_ref[t, chunk, 0], kv_ref[t, chunk, 1]
        return mem_ref[t - 3, 0], mem_ref[t - 3, 1]

    top = None
    for t in range(tiles):
        s = dot_nt(q, key_value(t)[0]) * SCALE
        if t == 0:
            s = jnp.where((col < row) & (base + col < length) | (col == row), s, BARRED)
        elif t == 1:
            s = jnp.where((base >= PAIR) & (base - PAIR + col < length), s, BARRED)
        elif t == 2:
            s = jnp.where((base >= 2 * PAIR) & (base - 2 * PAIR + col < length) & (row < col), s, BARRED)
        else:
            s = jnp.where(col // (PAIR // 4) < count, s, BARRED)
        scores[t] = s
        part = halves(jnp.maximum, s)
        top = part if top is None else jnp.maximum(top, part)
    top = jnp.max(top, axis=1, keepdims=True)
    total = None
    for t in range(tiles):
        e = jnp.exp2(scores[t] - top)
        scores[t] = e
        part = halves(jnp.add, e)
        total = part if total is None else total + part
    total = jnp.sum(total, axis=1, keepdims=True)
    inverse = 1.0 / total
    output = jnp.zeros((PAIR, HEAD), jnp.float32)
    for t in range(tiles):
        prob = scores[t] * inverse
        scores[t] = prob
        output += dot(prob.astype(jnp.bfloat16), key_value(t)[1])
    delta = jnp.sum(g.astype(jnp.float32) * output, axis=1, keepdims=True)
    grad = jnp.zeros((PAIR, HEAD), jnp.float32)
    for t in range(tiles):
        key, value = key_value(t)
        ds = scores[t] * (dot_nt(g, value) - delta)
        grad += dot(ds.astype(jnp.bfloat16), key)
    lse = top + jnp.log(total) * LOG2E
    lane = lax.broadcasted_iota(jnp.int32, (PAIR, HEAD), 1)
    both = jnp.where(lane == 0, lse, delta)
    return (grad * (1.0 / math.sqrt(HEAD))).astype(jnp.bfloat16), both.T[:8]


def owed(d, base, length, key, value, q, g, lse, delta):
    row, col = grid_of(PAIR, PAIR)
    live = base + row < length
    if d == 0:
        allowed = (row < col) & live | (row == col)
    elif d == 1:
        allowed = live & (base + PAIR < NX * NY * PAIR)
    else:
        allowed = live & (base + 2 * PAIR < NX * NY * PAIR) & (col < row)
    s = dot_nt(key, q) * SCALE - lse
    prob = jnp.where(allowed, jnp.exp2(jnp.where(allowed, s, BARRED)), 0.0)
    ds = prob * (dot_nt(value, g) - delta)
    return dot(ds.astype(jnp.bfloat16), q), dot(prob.astype(jnp.bfloat16), g)


def kernel(
    lengths, counts, lists, slots, q_ref, g_ref, k_ref, v_ref, poolk_ref, poolv_ref,
    gq_out, gk_out, gv_out,
    pool, staged, from_core, staged_z, from_z, picked, kv_ref, qg_ref, pieces, mem_ref, scores, stats, grads, sums,
    own_sem, a2a_send, a2a_recv, core_sems, z_send, z_recv, m_send, m_recv, hop_send, hop_recv, ring_send, ring_recv,
    stat_send, stat_recv, out_send, out_recv,
):
    zl, core, x, y, zh = place()
    user = zl * 2 + core
    head = x * NZ + zh
    above, below = [[device(zl, core, x, (y + s * d + NY) % NY, zh) for d in range(3)] for s in (1, -1)]
    peers = [device(zl, core, (x + a) % NX, y, (zh + b) % NZ) for a, b in GROUP]
    twin = device(zl, 1 - core, x, y, zh)
    line = [device((zl + a) % ZL, core, x, y, zh) for a in range(ZL)]
    loads = [
        pltpu.make_async_copy(poolk_ref, pool.at[0], own_sem.at[5]),
        pltpu.make_async_copy(poolv_ref, pool.at[1], own_sem.at[6]),
    ]
    for copy in loads:
        copy.start()
    greet(peers[1:] + above[1:] + below[1:] + [twin] + line[1:])
    ended = []

    def launch(copy):
        copy.start()
        ended.append(copy)
        return copy

    def shuffle(base, sources, into):
        out = []
        for i, (a, b) in enumerate(GROUP):
            part = columns(((x + a) % NX) * NZ + (zh + b) % NZ)
            for n, source in enumerate(sources):
                src, dst = source.at[0, :, part], into.at[0, x, n, pl.ds(pl.multiple_of(zh * ROWS, ROWS), ROWS)]
                if i == 0:
                    out.append(pltpu.make_async_copy(src, dst, own_sem.at[base + n]))
                    out[-1].start()
                else:
                    at = (base + n, i)
                    out.append(launch(remote(src, dst, a2a_send.at[at], a2a_recv.at[at], peers[i])))
        return out

    def arrived(copy, i):
        if i == 0:
            copy.wait()
        else:
            copy.wait_recv()

    def first_hop(moves, buf, lane, to, shift):
        out = []
        for a in range(NX):
            for i, (pa, pb) in enumerate(GROUP):
                if pa == a:
                    arrived(moves[2 * i], i)
                    arrived(moves[2 * i + 1], i)
            source = (x + NX - a) % NX
            sems = hop_send.at[lane, 0, a], hop_recv.at[lane, 0, a]
            out.append(launch(remote(buf.at[0, source], buf.at[1, (source + shift) % NX], *sems, to)))
        return out

    def second_hop(moves, buf, lane, to, before, shift):
        out = []
        for a in range(NX):
            moves[a].wait_recv()
            source = (x + NX - a + before) % NX
            sems = hop_send.at[lane, 1, a], hop_recv.at[lane, 1, a]
            out.append(launch(remote(buf.at[1, source], buf.at[2, (source + shift) % NX], *sems, to)))
        return out

    top, bottom = (y == NY - 1).astype(jnp.int32), (y == 0).astype(jnp.int32)

    kv_moves = shuffle(0, (k_ref, v_ref), kv_ref)

    for copy in loads:
        copy.wait()

    def slot_of(who, m):
        return slots[lists[m, who]]

    for z in range(ZL):
        for m in range(4):
            row = slot_of(z * 2 + (1 - core), m) % 8
            staged[z, 0, m] = pool[0, row]
            staged[z, 1, m] = pool[1, row]
    to_twin = remote(staged, from_core, core_sems.at[0], core_sems.at[1], twin)
    to_twin.start()
    to_twin.wait()
    for z in range(ZL):
        for m in range(4):
            slot = slot_of(z * 2 + core, m)
            mine = (slot // 8) % 2 == core
            staged_z[z, 0, m] = jnp.where(mine, pool[0, slot % 8], from_core[z, 0, m])
            staged_z[z, 1, m] = jnp.where(mine, pool[1, slot % 8], from_core[z, 1, m])
    z_moves = [
        launch(remote(staged_z.at[(zl + a) % ZL], from_z.at[zl], z_send.at[a], z_recv.at[a], line[a]))
        for a in range(1, ZL)
    ]
    from_z[zl] = staged_z[zl]

    kv_hops = first_hop(kv_moves, kv_ref, 0, above[1], top)

    for move in z_moves:
        move.wait_recv()
    for m in range(4):
        owner = slot_of(user, m) // 16
        picked[0, m] = from_z[owner, 0, m]
        picked[1, m] = from_z[owner, 1, m]
    m_moves = []
    for i, (a, b) in enumerate(GROUP):
        part = columns(((x + a) % NX) * NZ + (zh + b) % NZ)
        src, dst = picked.at[:, :, :, part], pieces.at[y, :, :, head]
        if i == 0:
            m_moves.append(pltpu.make_async_copy(src, dst, own_sem.at[4]))
            m_moves[-1].start()
        else:
            m_moves.append(launch(remote(src, dst, m_send.at[i], m_recv.at[i], peers[i])))

    qg_moves = shuffle(2, (q_ref, g_ref), qg_ref)
    kv_hops2 = second_hop(kv_hops, kv_ref, 0, above[1], bottom, top)

    for i, copy in enumerate(m_moves):
        arrived(copy, i)
    rising, falling = [], []
    for step in range(NY // 2):
        if step:
            rising[-1].wait_recv()
        piece = pieces.at[(y + NY - step) % NY]
        rising.append(launch(remote(piece, piece, ring_send.at[0, step], ring_recv.at[0, step], above[1])))
        if step < NY // 2 - 1:
            if step:
                falling[-1].wait_recv()
            piece = pieces.at[(y + step) % NY]
            falling.append(launch(remote(piece, piece, ring_send.at[1, step], ring_recv.at[1, step], below[1])))
        if step == 0:
            qg_hops = first_hop(qg_moves, qg_ref, 1, below[1], (NX - 1) * bottom)
    rising[-1].wait_recv()
    falling[-1].wait_recv()
    for piece in range(NY):
        for n in range(2):
            mem_ref[piece, n] = pieces[piece, n].reshape(PAIR, HEAD)
    for copy in kv_hops2:
        copy.wait_recv()

    length, count = lengths[user], counts[user]
    pos = lax.broadcasted_iota(jnp.int32, (PAIR, HEAD), 0)

    def cotangent(d, chunk, base):
        return jnp.where(pos + base + d * PAIR < length, qg_ref[d, chunk, 1], jnp.zeros((), jnp.bfloat16))

    def base_of(chunk):
        return (chunk * NY + y) * PAIR

    def chunk_at(a):
        return (x + NX - a) % NX

    outs = (gq_out, gk_out, gv_out)
    part = columns(head)

    def piece_out(n, a, b):
        half = (zh + b) % NZ
        chunk = chunk_at(a)
        return remote(
            grads.at[n, chunk, pl.ds(pl.multiple_of(half * ROWS, ROWS), ROWS)],
            outs[n].at[0, :, part],
            out_send.at[n, a, b],
            out_recv.at[n, a, b],
            device(zl, core, chunk, y, half),
        )

    def own_out(n):
        src = grads.at[n, x, pl.ds(pl.multiple_of(zh * ROWS, ROWS), ROWS)]
        return pltpu.make_async_copy(src, outs[n].at[0, :, part], own_sem.at[7 + n])

    def send_out(n, a):
        piece_out(n, a, 1).start()

        @pl.when(a == 0)
        def _():
            own_out(n).start()

        @pl.when(a != 0)
        def _():
            piece_out(n, a, 0).start()

    def stat_out(d, a):
        chunk = chunk_at(a)
        shift = (NX - 1) * (y < d).astype(jnp.int32)
        return remote(
            stats.at[0, chunk],
            stats.at[d, (chunk + shift) % NX],
            stat_send.at[d - 1, a],
            stat_recv.at[d - 1, a],
            below[d],
        )

    def attend_chunk(a, _):
        chunk = chunk_at(a)
        base = base_of(chunk)
        grad, both = attend(
            base, length, count, qg_ref[0, chunk, 0], cotangent(0, chunk, base), kv_ref, chunk, mem_ref, scores
        )
        grads[0, chunk] = grad
        stats[0, chunk] = both
        for d in (1, 2):
            stat_out(d, a).start()
        send_out(0, a)
        return 0

    def contribution(d, chunk):
        base = base_of(chunk)
        return owed(
            d, base, length, kv_ref[0, chunk, 0], kv_ref[0, chunk, 1], qg_ref[d, chunk, 0],
            cotangent(d, chunk, base), stats[d, chunk, 0:1], stats[d, chunk, 1:2],
        )

    def own_chunk(a, _):
        chunk = chunk_at(a)
        sums[0, chunk], sums[1, chunk] = contribution(0, chunk)
        return 0

    def ahead_chunk(a, _):
        chunk = chunk_at(a)
        gk, gv = sums[0, chunk], sums[1, chunk]
        for d in (1, 2):
            more_k, more_v = contribution(d, chunk)
            gk, gv = gk + more_k, gv + more_v
        grads[1, chunk] = (gk * (1.0 / math.sqrt(HEAD))).astype(jnp.bfloat16)
        grads[2, chunk] = gv.astype(jnp.bfloat16)
        send_out(1, a)
        send_out(2, a)
        return 0

    qg_hops2 = second_hop(qg_hops, qg_ref, 1, below[1], (NX - 1) * top, (NX - 1) * bottom)
    lax.fori_loop(0, NX, attend_chunk, 0)
    lax.fori_loop(0, NX, own_chunk, 0)
    for copy in qg_hops2:
        copy.wait_recv()
    for d in (1, 2):
        for a in range(NX):
            stat_out(d, a).wait_recv()
    lax.fori_loop(0, NX, ahead_chunk, 0)

    for n in range(3):
        own_out(n).wait()
        for i, (a, b) in enumerate(GROUP):
            if i:
                piece_out(n, a, b).wait()
    for d in (1, 2):
        for a in range(NX):
            stat_out(d, a).wait_send()
    for copy in ended:
        copy.wait_send()


def backward(lengths, counts, lists, slots, queries, grads, keys, values, poolk, poolv):
    bf16, f32 = jnp.bfloat16, jnp.float32
    out = jax.ShapeDtypeStruct(queries.shape, bf16)
    dma = pltpu.SemaphoreType.DMA
    rows = (8, H * HEAD)
    return pl.pallas_call(
        kernel,
        name="backward",
        out_shape=(out,) * 3,
        in_specs=[SMEM] * 4 + [HBM] * 6,
        out_specs=(ANY,) * 3,
        scratch_shapes=[
            pltpu.VMEM((2, 8, *rows), bf16),
            pltpu.VMEM((ZL, 2, 4, *rows), bf16),
            pltpu.VMEM((ZL, 2, 4, *rows), bf16),
            pltpu.VMEM((ZL, 2, 4, *rows), bf16),
            pltpu.VMEM((ZL, 2, 4, *rows), bf16),
            pltpu.VMEM((2, 4, *rows), bf16),
            pltpu.VMEM((3, NX, 2, PAIR, HEAD), bf16),
            pltpu.VMEM((3, NX, 2, PAIR, HEAD), bf16),
            pltpu.VMEM((NY, 2, 4, H, 8, HEAD), bf16),
            pltpu.VMEM((NY, 2, PAIR, HEAD), bf16),
            pltpu.VMEM((3 + NY, PAIR, PAIR), f32),
            pltpu.VMEM((3, NX, 8, PAIR), f32),
            pltpu.VMEM((3, NX, PAIR, HEAD), bf16),
            pltpu.VMEM((2, NX, PAIR, HEAD), f32),
            dma((10,)),
            dma((4, 8)),
            dma((4, 8)),
            dma((2,)),
            dma((ZL,)),
            dma((ZL,)),
            dma((8,)),
            dma((8,)),
            dma((2, 2, NX)),
            dma((2, 2, NX)),
            dma((2, 4)),
            dma((2, 4)),
            dma((2, NX)),
            dma((2, NX)),
            dma((3, NX, NZ)),
            dma((3, NX, NZ)),
        ],
        compiler_params=pltpu.CompilerParams(
            collective_id=0, has_side_effects=True, vmem_limit_bytes=40 << 20
        ),
    )(lengths, counts, lists, slots, queries, grads, keys, values, poolk, poolv)


def on_device(queries, keys, values, grad_out, mem_keys, mem_values, seq_lengths, mem_counts, block_lists, block_slots):
    return backward(
        seq_lengths, mem_counts, block_lists.T, block_slots, queries, grad_out, keys, values, mem_keys, mem_values
    )


def solution(mesh):
    rows = P("dp", "seq", None)
    return jax.shard_map(
        on_device,
        mesh=mesh,
        in_specs=(rows,) * 6 + (P(),) * 4,
        out_specs=(rows,) * 3,
        check_vma=False,
    )
```

time: 659 us -> 114 us (0.17)
  the two profiles are of different devices: /device:TPU:168 before, /device:TPU:120 now
where the time goes in v2:
time: 114 us
  Pallas kernels  104 us (91%)
  local copies, waits for them, and re-layouts  9.06 us (8%)
    pallas_call x1, Pallas kernels, backward(): pl.pallas_call(kernel, name='backward', out_shape=(out,) * 3, in_specs=[S...  104 us
    unnamed x23, local copies, waits for them, and re-layouts  9.06 us

profile of v2, /device:TPU:120, one launch (start us, length us, event | category | flops | bytes accessed | tf_op | source)
XLA Modules:
  0.0 113.8 jit_solution(7734523252396621807)
XLA Ops:
  0.6 0.0 copy-start.9
  0.6 0.0 copy-start.8
  0.7 0.0 copy-start.7
  0.7 0.6 copy-done.9
  1.3 0.0 copy-done.8
  1.3 0.0 copy-done.7
  1.3 0.0 copy-start
  1.3 0.9 copy-done
  2.3 0.0 copy-start.1
  2.3 0.9 copy-done.1
  3.2 0.0 copy-start.2
  3.2 0.9 copy-done.2
  4.2 0.0 copy-start.3
  4.2 0.9 copy-done.3
  5.1 0.0 copy-start.4
  5.1 0.9 copy-done.4
  6.0 0.0 copy-start.5
  6.0 0.9 copy-done.5
  6.9 0.0 copy-start.6
  6.9 0.7 copy-done.6
  7.6 104.1 %backward.1 = (bf16[1,128,1024]{2,1,0:T(8,128)(2,1)S(1)}, bf16[1,128,1024]{2,1,0:T(8,128)(2,1)S(1)}, bf16[1,128,1024]{2,1,0:T(8,128)(2,1)S(1)}) custom-call(s32[8]{0:T(128)S(1)} %copy-done.7, s32[8]{0:T(128)S(1)} %copy-done.8, s32[4,8]{1,0:T(4,128)S(1)} %bitcast.1, s32[64]{0:T(128)S(1)} %copy-done.9, bf16[1,128,1024]{2,1,0:T(8,128)(2,1)S(1)} %copy-done, ...), custom_call_target="tpu_custom_call" | custom-call | tf_op jit(solution)/shard_map/backward/pallas_call | solution.py:394
  111.7 0.7 copy.16
  112.4 0.7 copy.17
  113.1 0.7 copy.18
Async XLA Ops:
  0.6 0.7 copy-start.9
  0.6 0.7 copy-start.8
  0.7 0.7 copy-start.7
  1.3 0.9 copy-start
  2.3 0.9 copy-start.1
  3.2 0.9 copy-start.2
  4.2 0.9 copy-start.3
  5.1 0.9 copy-start.4
  6.0 0.9 copy-start.5
  6.9 0.7 copy-start.6

commit v3 on v2

v3 whole, which is shorter than its diff:
```python
import functools
import math

import jax
import jax.numpy as jnp
from jax import lax
from jax.experimental import pallas as pl
from jax.experimental.pallas import tpu as pltpu
from jax.sharding import PartitionSpec as P

MESH = pl.DeviceIdType.MESH
ANY = pl.BlockSpec(memory_space=pl.ANY)
HBM = pl.BlockSpec(memory_space=pltpu.HBM)
SMEM = pl.BlockSpec(memory_space=pltpu.SMEM)
H = 8
WINDOW = 512
BLK = 512
NX, NY, NZ, ZL = 4, 8, 2, 4
ROWS, HEAD = 128, 128
PAIR = NZ * ROWS
GROUP = [(a, b) for a in range(NX) for b in range(NZ)]
LOG2E = math.log2(math.e)
BARRED = -1e30
UP = 4


def place():
    dp, seq = lax.axis_index("dp"), lax.axis_index("seq")
    return dp // 2, dp % 2, seq // (NY * NZ), (seq // NZ) % NY, seq % NZ


def device(zl, core, x, y, zh):
    return (zl * 2 + core, (x * NY + y) * NZ + zh)


def announce(partners):
    for partner in partners:
        pl.semaphore_signal(
            pltpu.get_barrier_semaphore(), inc=1, device_id=partner, device_id_type=MESH
        )


def remote(src, dst, send, recv, to):
    return pltpu.make_async_remote_copy(
        src_ref=src, dst_ref=dst, send_sem=send, recv_sem=recv, device_id=to, device_id_type=MESH
    )


def columns(head):
    return pl.ds(pl.multiple_of(head * HEAD, HEAD), HEAD)

TILES = 3 + 4 * BLK // PAIR
SCALE = LOG2E / math.sqrt(HEAD)
NT = (((1,), (1,)), ((), ()))


def dot_nt(a, b):
    return lax.dot_general(a, b, NT, preferred_element_type=jnp.float32)


def dot(a, b):
    return jnp.dot(a, b, preferred_element_type=jnp.float32)


def halves(op, tile):
    return op(tile[:, :HEAD], tile[:, HEAD:])


def grid_of(rows, cols):
    return tuple(lax.broadcasted_iota(jnp.int32, (rows, cols), i) for i in range(2))


def weigh(base, length, count, q, key_of, weights):
    row, col = grid_of(PAIR, PAIR)
    top = None
    for t in range(TILES):
        s = dot_nt(q, key_of(t)) * SCALE
        if t == 0:
            s = jnp.where((col < row) & (base + col < length) | (col == row), s, BARRED)
        elif t == 1:
            s = jnp.where((base >= PAIR) & (base - PAIR + col < length), s, BARRED)
        elif t == 2:
            s = jnp.where((base >= 2 * PAIR) & (base - 2 * PAIR + col < length) & (row < col), s, BARRED)
        weights[t] = s
        part = halves(jnp.maximum, s)
        if t >= 3:
            part = jnp.where(block_of(t) < count, part, BARRED)
        top = part if top is None else jnp.maximum(top, part)
    top = jnp.max(top, axis=1, keepdims=True)
    total = None
    for t in range(TILES):
        base_line = top if t < 3 else top + jnp.where(block_of(t) < count, 0.0, -BARRED)
        e = jnp.exp2(weights[t] - base_line)
        weights[t] = e
        part = halves(jnp.add, e)
        total = part if total is None else total + part
    return top, jnp.sum(total, axis=1, keepdims=True)


def block_of(t):
    return (t - 3) // (BLK // PAIR)


def answer(top, total, g, key_of, value_of, weights):
    inverse = 1.0 / total
    output = jnp.zeros((PAIR, HEAD), jnp.float32)
    for t in range(TILES):
        prob = weights[t] * inverse
        output += dot(prob.astype(jnp.bfloat16), value_of(t))
    delta = jnp.sum(g.astype(jnp.float32) * output, axis=1, keepdims=True)
    grad = jnp.zeros((PAIR, HEAD), jnp.float32)
    for t in range(TILES):
        ds = (weights[t] * inverse) * (dot_nt(g, value_of(t)) - delta)
        grad += dot(ds.astype(jnp.bfloat16), key_of(t))
    lse = top + jnp.log(total) * LOG2E
    lane = lax.broadcasted_iota(jnp.int32, (PAIR, HEAD), 1)
    both = jnp.where(lane == 0, lse, delta)
    return (grad * (1.0 / math.sqrt(HEAD))).astype(jnp.bfloat16), both.T[:8]


def owed(d, base, length, key, value, q, g, lse, delta):
    row, col = grid_of(PAIR, PAIR)
    live = base + row < length
    if d == 0:
        allowed = (row < col) & live | (row == col)
    elif d == 1:
        allowed = live & (base + PAIR < NX * NY * PAIR)
    else:
        allowed = live & (base + 2 * PAIR < NX * NY * PAIR) & (col < row)
    s = dot_nt(key, q) * SCALE - lse
    prob = jnp.where(allowed, jnp.exp2(jnp.where(allowed, s, BARRED)), 0.0)
    ds = prob * (dot_nt(value, g) - delta)
    return dot(ds.astype(jnp.bfloat16), q), dot(prob.astype(jnp.bfloat16), g)


def kernel(
    lengths, counts, lists, slots, q_ref, g_ref, k_ref, v_ref, poolk_ref, poolv_ref,
    gq_out, gk_out, gv_out,
    pool0, pool1, staged, from_core, staged_z, from_z0, from_z1, picked, kv_ref, qg_ref, pieces, mem_ref, weights, tops, stats, grads, sums,
    own_sem, a2a_send, a2a_recv, core_sems, z_send, z_recv, m_send, m_recv, hop_send, hop_recv, ring_send, ring_recv,
    stat_send, stat_recv, out_send, out_recv,
):
    zl, core, x, y, zh = place()
    user = zl * 2 + core
    pool, from_z = (pool0, pool1), (from_z0, from_z1)
    head = x * NZ + zh
    above, below = [[device(zl, core, x, (y + s * d + NY) % NY, zh) for d in range(3)] for s in (1, -1)]
    peers = [device(zl, core, (x + a) % NX, y, (zh + b) % NZ) for a, b in GROUP]
    twin = device(zl, 1 - core, x, y, zh)
    line = [device((zl + a) % ZL, core, x, y, zh) for a in range(ZL)]
    loads = [
        pltpu.make_async_copy(poolk_ref, pool0, own_sem.at[5]),
        pltpu.make_async_copy(poolv_ref, pool1, own_sem.at[6]),
    ]
    for copy in loads:
        copy.start()
    partners = peers[1:] + above[1:] + below[1:] + [twin] + line[1:]
    announce(partners)
    ended = []

    def launch(copy):
        copy.start()
        ended.append(copy)
        return copy

    def arrived(copy, i):
        if i == 0:
            copy.wait()
        else:
            copy.wait_recv()

    def chunk_at(a):
        return (x + NX - a) % NX

    class Stream:
        def __init__(self, lane, sources, buf, to, shift, before):
            self.lane, self.sources, self.buf, self.to = lane, sources, buf, to
            self.shift, self.before = shift, before
            self.moves, self.hops = {}, {}

        def shuffle(self, a):
            out = []
            for b in range(NZ):
                i = a * NZ + b
                part = columns(((x + a) % NX) * NZ + (zh + b) % NZ)
                for n, source in enumerate(self.sources):
                    src = source.at[0, :, part]
                    dst = self.buf.at[0, x, n, pl.ds(pl.multiple_of(zh * ROWS, ROWS), ROWS)]
                    k = 2 * self.lane + n
                    if i == 0:
                        out.append((pltpu.make_async_copy(src, dst, own_sem.at[k]), i))
                        out[-1][0].start()
                    else:
                        out.append((launch(remote(src, dst, a2a_send.at[k, i], a2a_recv.at[k, i], peers[i])), i))
            self.moves[a] = out

        def hop(self, step, a):
            if step == 0:
                for copy, i in self.moves[a]:
                    arrived(copy, i)
                source = chunk_at(a)
            else:
                self.hops[0, a].wait_recv()
                source = (chunk_at(a) + self.before) % NX
            sems = hop_send.at[self.lane, step, a], hop_recv.at[self.lane, step, a]
            src, dst = self.buf.at[step, source], self.buf.at[step + 1, (source + self.shift) % NX]
            self.hops[step, a] = launch(remote(src, dst, *sems, self.to))

        def landed(self, a):
            self.hops[1, a].wait_recv()

    top, bottom = (y == NY - 1).astype(jnp.int32), (y == 0).astype(jnp.int32)
    kv = Stream(0, (k_ref, v_ref), kv_ref, above[1], top, bottom)
    qg = Stream(1, (q_ref, g_ref), qg_ref, below[1], (NX - 1) * bottom, (NX - 1) * top)

    def slot_of(who, m):
        return slots[lists[m, who]]

    for n in range(2):
        loads[n].wait()
        for z in range(ZL):
            for m in range(4):
                staged[n, z, m] = pool[n][slot_of(z * 2 + (1 - core), m) % 8]
    pl.semaphore_wait(pltpu.get_barrier_semaphore(), len(partners))

    def to_twin(n):
        return remote(staged.at[n], from_core.at[n], core_sems.at[0, n], core_sems.at[1, n], twin)

    def send_twin():
        for n in range(2):
            launch(to_twin(n))

    def stage_z(n):
        to_twin(n).wait_recv()
        for z in range(ZL):
            for m in range(4):
                slot = slot_of(z * 2 + core, m)
                mine = (slot // 8) % 2 == core
                staged_z[n, z, m] = jnp.where(mine, pool[n][slot % 8], from_core[n, z, m])
        from_z[n][zl] = staged_z[n, zl]

    def z_move(n, a):
        src, dst = staged_z.at[n, (zl + a) % ZL], from_z[n].at[zl]
        return remote(src, dst, z_send.at[n, a], z_recv.at[n, a], line[a])

    def send_z(n):
        for a in range(1, ZL):
            launch(z_move(n, a))

    def m_move(n, i):
        a, b = GROUP[i]
        columns_to = columns(((x + a) % NX) * NZ + (zh + b) % NZ)
        src, dst = picked.at[n, :, :, columns_to], pieces.at[y, n, :, head]
        if i == 0:
            return pltpu.make_async_copy(src, dst, own_sem.at[4 + 6 * n])
        return remote(src, dst, m_send.at[n, i], m_recv.at[n, i], peers[i])

    def send_memory(n):
        for a in range(1, ZL):
            z_move(n, a).wait_recv()
        for m in range(4):
            picked[n, m] = from_z[n][slot_of(user, m) // 16, m]
        m_move(n, 0).start()
        for i in range(1, len(GROUP)):
            launch(m_move(n, i))

    rising, falling = ([], []), ([], [])

    def ring(n, step):
        if step == 0:
            for i in range(len(GROUP)):
                arrived(m_move(n, i), i)
        if step:
            rising[n][-1].wait_recv()
        if step < UP:
            piece = pieces.at[(y + NY - step) % NY, n]
            sems = ring_send.at[n, 0, step], ring_recv.at[n, 0, step]
            rising[n].append(launch(remote(piece, piece, *sems, above[1])))
        if step and step <= NY - 1 - UP:
            falling[n][-1].wait_recv()
        if step < NY - 1 - UP:
            piece = pieces.at[(y + step) % NY, n]
            sems = ring_send.at[n, 1, step], ring_recv.at[n, 1, step]
            falling[n].append(launch(remote(piece, piece, *sems, below[1])))

    kv.shuffle(0)
    kv.shuffle(1)
    kv.shuffle(2)
    kv.shuffle(3)
    send_twin()
    stage_z(0)
    stage_z(1)
    kv.hop(0, 0)
    kv.hop(0, 1)
    qg.shuffle(0)
    qg.shuffle(1)
    kv.hop(0, 2)
    kv.hop(0, 3)
    qg.shuffle(2)
    qg.shuffle(3)
    send_z(0)
    send_z(1)
    kv.hop(1, 0)
    kv.hop(1, 1)
    kv.hop(1, 2)
    qg.hop(0, 0)
    qg.hop(0, 1)
    kv.hop(1, 3)
    qg.hop(0, 2)
    qg.hop(0, 3)
    send_memory(0)
    send_memory(1)
    ring(0, 0)
    ring(1, 0)
    ring(0, 1)
    ring(1, 1)
    qg.hop(1, 0)
    ring(0, 2)
    ring(1, 2)
    qg.hop(1, 1)
    ring(0, 3)
    ring(1, 3)

    def settle(n):
        ring(n, UP)
        for piece in range(NY):
            for m in range(4):
                size = PAIR // 4
                mem_ref[m, n, piece * size : (piece + 1) * size] = pieces[piece, n, m].reshape(size, HEAD)

    settle(0)
    for a in range(NX):
        kv.landed(a)

    length, count = lengths[user], counts[user]
    pos = lax.broadcasted_iota(jnp.int32, (PAIR, HEAD), 0)

    def cotangent(d, chunk, base):
        return jnp.where(pos + base + d * PAIR < length, qg_ref[d, chunk, 1], jnp.zeros((), jnp.bfloat16))

    def base_of(chunk):
        return (chunk * NY + y) * PAIR

    outs = (gq_out, gk_out, gv_out)
    part = columns(head)

    def piece_out(n, a, b):
        half = (zh + b) % NZ
        chunk = chunk_at(a)
        return remote(
            grads.at[n, chunk, pl.ds(pl.multiple_of(half * ROWS, ROWS), ROWS)],
            outs[n].at[0, :, part],
            out_send.at[n, a, b],
            out_recv.at[n, a, b],
            device(zl, core, chunk, y, half),
        )

    def own_out(n):
        src = grads.at[n, x, pl.ds(pl.multiple_of(zh * ROWS, ROWS), ROWS)]
        return pltpu.make_async_copy(src, outs[n].at[0, :, part], own_sem.at[7 + n])

    def send_out(n, a):
        piece_out(n, a, 1).start()

        @pl.when(a == 0)
        def _():
            own_out(n).start()

        @pl.when(a != 0)
        def _():
            piece_out(n, a, 0).start()

    def stat_out(d, a):
        chunk = chunk_at(a)
        shift = (NX - 1) * (y < d).astype(jnp.int32)
        return remote(
            stats.at[0, chunk],
            stats.at[d, (chunk + shift) % NX],
            stat_send.at[d - 1, a],
            stat_recv.at[d - 1, a],
            below[d],
        )

    def tile_of(n, chunk):
        def one(t):
            if t < 3:
                return kv_ref[t, chunk, n]
            half = (t - 3) % (BLK // PAIR)
            return mem_ref[block_of(t), n, half * PAIR : (half + 1) * PAIR]

        return one

    def weigh_chunk(a, _):
        chunk = chunk_at(a)
        top, total = weigh(
            base_of(chunk), length, count, qg_ref[0, chunk, 0], tile_of(0, chunk), weights.at[chunk]
        )
        tops[0, chunk] = jnp.broadcast_to(top, (PAIR, HEAD))
        tops[1, chunk] = jnp.broadcast_to(total, (PAIR, HEAD))
        return 0

    def answer_chunk(a, _):
        chunk = chunk_at(a)
        grad, both = answer(
            tops[0, chunk][:, :1], tops[1, chunk][:, :1], cotangent(0, chunk, base_of(chunk)),
            tile_of(0, chunk), tile_of(1, chunk), weights.at[chunk],
        )
        grads[0, chunk] = grad
        stats[0, chunk] = both
        for d in (1, 2):
            stat_out(d, a).start()
        send_out(0, a)
        return 0

    def contribution(d, chunk):
        base = base_of(chunk)
        return owed(
            d, base, length, kv_ref[0, chunk, 0], kv_ref[0, chunk, 1], qg_ref[d, chunk, 0],
            cotangent(d, chunk, base), stats[d, chunk, 0:1], stats[d, chunk, 1:2],
        )

    def own_chunk(a, _):
        chunk = chunk_at(a)
        sums[0, chunk], sums[1, chunk] = contribution(0, chunk)
        return 0

    def ahead_chunk(a, _):
        chunk = chunk_at(a)
        gk, gv = sums[0, chunk], sums[1, chunk]
        for d in (1, 2):
            more_k, more_v = contribution(d, chunk)
            gk, gv = gk + more_k, gv + more_v
        grads[1, chunk] = (gk * (1.0 / math.sqrt(HEAD))).astype(jnp.bfloat16)
        grads[2, chunk] = gv.astype(jnp.bfloat16)
        send_out(1, a)
        send_out(2, a)
        return 0

    lax.fori_loop(0, 2, weigh_chunk, 0)
    qg.hop(1, 2)
    lax.fori_loop(2, 4, weigh_chunk, 0)
    qg.hop(1, 3)
    settle(1)
    lax.fori_loop(0, 4, answer_chunk, 0)
    lax.fori_loop(0, NX, own_chunk, 0)
    for d in (1, 2):
        for a in range(NX):
            stat_out(d, a).wait_recv()
    turned = (y >= NY - 2).astype(jnp.int32)
    for a in range(NX):
        qg.landed(a)
        ahead_chunk((a + turned) % NX, 0)

    for n in range(3):
        own_out(n).wait()
        for i, (a, b) in enumerate(GROUP):
            if i:
                piece_out(n, a, b).wait()
    for d in (1, 2):
        for a in range(NX):
            stat_out(d, a).wait_send()
    for copy in ended:
        copy.wait_send()


def backward(lengths, counts, lists, slots, queries, grads, keys, values, poolk, poolv):
    bf16, f32 = jnp.bfloat16, jnp.float32
    out = jax.ShapeDtypeStruct(queries.shape, bf16)
    dma = pltpu.SemaphoreType.DMA
    rows = (8, H * HEAD)
    return pl.pallas_call(
        kernel,
        name="backward",
        out_shape=(out,) * 3,
        in_specs=[SMEM] * 4 + [HBM] * 6,
        out_specs=(ANY,) * 3,
        scratch_shapes=[
            pltpu.VMEM((8, *rows), bf16),
            pltpu.VMEM((8, *rows), bf16),
            pltpu.VMEM((2, ZL, 4, *rows), bf16),
            pltpu.VMEM((2, ZL, 4, *rows), bf16),
            pltpu.VMEM((2, ZL, 4, *rows), bf16),
            pltpu.VMEM((ZL, 4, *rows), bf16),
            pltpu.VMEM((ZL, 4, *rows), bf16),
            pltpu.VMEM((2, 4, *rows), bf16),
            pltpu.VMEM((3, NX, 2, PAIR, HEAD), bf16),
            pltpu.VMEM((3, NX, 2, PAIR, HEAD), bf16),
            pltpu.VMEM((NY, 2, 4, H, 8, HEAD), bf16),
            pltpu.VMEM((4, 2, BLK, HEAD), bf16),
            pltpu.VMEM((NX, TILES, PAIR, PAIR), f32),
            pltpu.VMEM((2, NX, PAIR, HEAD), f32),
            pltpu.VMEM((3, NX, 8, PAIR), f32),
            pltpu.VMEM((3, NX, PAIR, HEAD), bf16),
            pltpu.VMEM((2, NX, PAIR, HEAD), f32),
            dma((11,)),
            dma((4, 8)),
            dma((4, 8)),
            dma((2, 2)),
            dma((2, ZL)),
            dma((2, ZL)),
            dma((2, 8)),
            dma((2, 8)),
            dma((2, 2, NX)),
            dma((2, 2, NX)),
            dma((2, 2, UP)),
            dma((2, 2, UP)),
            dma((2, NX)),
            dma((2, NX)),
            dma((3, NX, NZ)),
            dma((3, NX, NZ)),
        ],
        compiler_params=pltpu.CompilerParams(
            collective_id=0, has_side_effects=True, vmem_limit_bytes=60 << 20
        ),
    )(lengths, counts, lists, slots, queries, grads, keys, values, poolk, poolv)


def finish_kernel(*refs):
    for n in range(3):
        refs[3 + n][...] = refs[n][...]


def finish(*parts):
    whole = pl.BlockSpec(memory_space=pltpu.VMEM)
    return pl.pallas_call(
        finish_kernel,
        name="finish",
        out_shape=tuple(jax.ShapeDtypeStruct(part.shape, part.dtype) for part in parts),
        in_specs=[whole] * 3,
        out_specs=(whole,) * 3,
    )(*parts)


def on_device(queries, keys, values, grad_out, mem_keys, mem_values, seq_lengths, mem_counts, block_lists, block_slots):
    parts = backward(
        seq_lengths, mem_counts, block_lists.T, block_slots, queries, grad_out, keys, values, mem_keys, mem_values
    )
    return finish(*parts)


def solution(mesh):
    rows = P("dp", "seq", None)
    return jax.shard_map(
        on_device,
        mesh=mesh,
        in_specs=(rows,) * 6 + (P(),) * 4,
        out_specs=(rows,) * 3,
        check_vma=False,
    )
```

time: 114 us -> 102 us (0.89)
  the two profiles are of different devices: /device:TPU:120 before, /device:TPU:200 now
where the time goes in v3:
time: 102 us
  Pallas kernels  101 us (99%)
    pallas_call x1, Pallas kernels, backward(): pl.pallas_call(kernel, name='backward', out_shape=(out,) * 3, in_specs=[S...  99.2 us

profile of v3, /device:TPU:200, one launch (start us, length us, event | category | flops | bytes accessed | tf_op | source)
XLA Modules:
  0.0 101.8 jit_solution(9971328890294674350)
XLA Ops:
  0.6 99.2 %backward.1 = (bf16[1,128,1024]{2,1,0:T(8,128)(2,1)}, bf16[1,128,1024]{2,1,0:T(8,128)(2,1)}, bf16[1,128,1024]{2,1,0:T(8,128)(2,1)}) custom-call(s32[8]{0:T(128)} %lengths.1, s32[8]{0:T(128)} %counts.1, s32[4,8]{1,0:T(4,128)} %bitcast.1, s32[64]{0:T(128)} %slots.1, bf16[1,128,1024]{2,1,0:T(8,128)(2,1)} %q_ref.1, bf16[1,128,1024]{2,1,0:T(8,128)(2,1)} %g_ref.1, ...), custom_call_target="tpu_custom_call" | custom-call | tf_op jit(solution)/shard_map/backward/pallas_call | solution.py:471
  99.8 2.0 %finish.1 = (bf16[1,128,1024]{2,1,0:T(8,128)(2,1)}, bf16[1,128,1024]{2,1,0:T(8,128)(2,1)}, bf16[1,128,1024]{2,1,0:T(8,128)(2,1)}) custom-call(bf16[1,128,1024]{2,1,0:T(8,128)(2,1)} %get-tuple-element.6.refs_0_, bf16[1,128,1024]{2,1,0:T(8,128)(2,1)} %get-tuple-element.7.refs_1_, bf16[1,128,1024]{2,1,0:T(8,128)(2,1)} %get-tuple-element.8.refs_2_), custom_call_target="tpu_custom_call" | custom-call | tf_op jit(solution)/shard_map/finish/pallas_call | solution.py:525

commit v4 on v3

--- a/solution.py
+++ b/solution.py
@@ -94,14 +94,19 @@
         weights[t] = e
         part = halves(jnp.add, e)
         total = part if total is None else total + part
-    return top, jnp.sum(total, axis=1, keepdims=True)
+    total = jnp.sum(total, axis=1, keepdims=True)
+    return top, total, along_lanes(top + jnp.log(total) * LOG2E)
+
+
+def along_lanes(column):
+    return jnp.broadcast_to(column, (PAIR, HEAD)).T[:8]
 
 
 def block_of(t):
     return (t - 3) // (BLK // PAIR)
 
 
-def answer(top, total, g, key_of, value_of, weights):
+def answer(total, g, key_of, value_of, weights):
     inverse = 1.0 / total
     output = jnp.zeros((PAIR, HEAD), jnp.float32)
     for t in range(TILES):
@@ -112,13 +117,10 @@
     for t in range(TILES):
         ds = (weights[t] * inverse) * (dot_nt(g, value_of(t)) - delta)
         grad += dot(ds.astype(jnp.bfloat16), key_of(t))
-    lse = top + jnp.log(total) * LOG2E
-    lane = lax.broadcasted_iota(jnp.int32, (PAIR, HEAD), 1)
-    both = jnp.where(lane == 0, lse, delta)
-    return (grad * (1.0 / math.sqrt(HEAD))).astype(jnp.bfloat16), both.T[:8]
-
-
-def owed(d, base, length, key, value, q, g, lse, delta):
+    return (grad * (1.0 / math.sqrt(HEAD))).astype(jnp.bfloat16), along_lanes(delta)
+
+
+def seen_again(d, base, length, key, q, lse):
     row, col = grid_of(PAIR, PAIR)
     live = base + row < length
     if d == 0:
@@ -128,15 +130,13 @@
     else:
         allowed = live & (base + 2 * PAIR < NX * NY * PAIR) & (col < row)
     s = dot_nt(key, q) * SCALE - lse
-    prob = jnp.where(allowed, jnp.exp2(jnp.where(allowed, s, BARRED)), 0.0)
-    ds = prob * (dot_nt(value, g) - delta)
-    return dot(ds.astype(jnp.bfloat16), q), dot(prob.astype(jnp.bfloat16), g)
+    return jnp.where(allowed, jnp.exp2(jnp.where(allowed, s, BARRED)), 0.0)
 
 
 def kernel(
     lengths, counts, lists, slots, q_ref, g_ref, k_ref, v_ref, poolk_ref, poolv_ref,
     gq_out, gk_out, gv_out,
-    pool0, pool1, staged, from_core, staged_z, from_z0, from_z1, picked, kv_ref, qg_ref, pieces, mem_ref, weights, tops, stats, grads, sums,
+    pool0, pool1, staged, from_core, staged_z, from_z0, from_z1, picked, kv_ref, qg_ref, pieces, mem_ref, weights, totals, stats, grads, probs,
     own_sem, a2a_send, a2a_recv, core_sems, z_send, z_recv, m_send, m_recv, hop_send, hop_recv, ring_send, ring_recv,
     stat_send, stat_recv, out_send, out_recv,
 ):
@@ -370,16 +370,21 @@
         def _():
             piece_out(n, a, 0).start()
 
-    def stat_out(d, a):
+    def stat_out(kind, d, a):
         chunk = chunk_at(a)
         shift = (NX - 1) * (y < d).astype(jnp.int32)
-        return remote(
-            stats.at[0, chunk],
-            stats.at[d, (chunk + shift) % NX],
-            stat_send.at[d - 1, a],
-            stat_recv.at[d - 1, a],
-            below[d],
-        )
+        sems = stat_send.at[kind, d - 1, a], stat_recv.at[kind, d - 1, a]
+        return remote(stats.at[kind, 0, chunk], stats.at[kind, d, (chunk + shift) % NX], *sems, below[d])
+
+    def share(kind, chunk, a, stat):
+        stats[kind, 0, chunk] = stat
+        for d in (1, 2):
+            stat_out(kind, d, a).start()
+
+    def shared(kind):
+        for d in (1, 2):
+            for a in range(NX):
+                stat_out(kind, d, a).wait_recv()
 
     def tile_of(n, chunk):
         def one(t):
@@ -392,48 +397,47 @@
 
     def weigh_chunk(a, _):
         chunk = chunk_at(a)
-        top, total = weigh(
+        _, total, lse = weigh(
             base_of(chunk), length, count, qg_ref[0, chunk, 0], tile_of(0, chunk), weights.at[chunk]
         )
-        tops[0, chunk] = jnp.broadcast_to(top, (PAIR, HEAD))
-        tops[1, chunk] = jnp.broadcast_to(total, (PAIR, HEAD))
+        totals[chunk] = jnp.broadcast_to(total, (PAIR, HEAD))
+        share(0, chunk, a, lse)
         return 0
 
     def answer_chunk(a, _):
         chunk = chunk_at(a)
-        grad, both = answer(
-            tops[0, chunk][:, :1], tops[1, chunk][:, :1], cotangent(0, chunk, base_of(chunk)),
+        grad, delta = answer(
+            totals[chunk][:, :1], cotangent(0, chunk, base_of(chunk)),
             tile_of(0, chunk), tile_of(1, chunk), weights.at[chunk],
         )
         grads[0, chunk] = grad
-        stats[0, chunk] = both
-        for d in (1, 2):
-            stat_out(d, a).start()
+        share(1, chunk, a, delta)
         send_out(0, a)
         return 0
 
-    def contribution(d, chunk):
+    def value_chunk(a):
+        chunk = chunk_at(a)
         base = base_of(chunk)
-        return owed(
-            d, base, length, kv_ref[0, chunk, 0], kv_ref[0, chunk, 1], qg_ref[d, chunk, 0],
-            cotangent(d, chunk, base), stats[d, chunk, 0:1], stats[d, chunk, 1:2],
-        )
-
-    def own_chunk(a, _):
+        gv = jnp.zeros((PAIR, HEAD), jnp.float32)
+        for d in range(3):
+            prob = seen_again(
+                d, base, length, kv_ref[0, chunk, 0], qg_ref[d, chunk, 0], stats[0, d, chunk, 0:1]
+            )
+            probs[chunk, d] = prob
+            gv += dot(prob.astype(jnp.bfloat16), cotangent(d, chunk, base))
+        grads[2, chunk] = gv.astype(jnp.bfloat16)
+        send_out(2, a)
+
+    def key_chunk(a, _):
         chunk = chunk_at(a)
-        sums[0, chunk], sums[1, chunk] = contribution(0, chunk)
-        return 0
-
-    def ahead_chunk(a, _):
-        chunk = chunk_at(a)
-        gk, gv = sums[0, chunk], sums[1, chunk]
-        for d in (1, 2):
-            more_k, more_v = contribution(d, chunk)
-            gk, gv = gk + more_k, gv + more_v
+        base = base_of(chunk)
+        gk = jnp.zeros((PAIR, HEAD), jnp.float32)
+        for d in range(3):
+            dprob = dot_nt(kv_ref[0, chunk, 1], cotangent(d, chunk, base))
+            ds = probs[chunk, d] * (dprob - stats[1, d, chunk, 0:1])
+            gk += dot(ds.astype(jnp.bfloat16), qg_ref[d, chunk, 0])
         grads[1, chunk] = (gk * (1.0 / math.sqrt(HEAD))).astype(jnp.bfloat16)
-        grads[2, chunk] = gv.astype(jnp.bfloat16)
         send_out(1, a)
-        send_out(2, a)
         return 0
 
     lax.fori_loop(0, 2, weigh_chunk, 0)
@@ -442,23 +446,23 @@
     qg.hop(1, 3)
     settle(1)
     lax.fori_loop(0, 4, answer_chunk, 0)
-    lax.fori_loop(0, NX, own_chunk, 0)
-    for d in (1, 2):
-        for a in range(NX):
-            stat_out(d, a).wait_recv()
+    shared(0)
     turned = (y >= NY - 2).astype(jnp.int32)
     for a in range(NX):
         qg.landed(a)
-        ahead_chunk((a + turned) % NX, 0)
+        value_chunk((a + turned) % NX)
+    shared(1)
+    lax.fori_loop(0, NX, key_chunk, 0)
 
     for n in range(3):
         own_out(n).wait()
         for i, (a, b) in enumerate(GROUP):
             if i:
                 piece_out(n, a, b).wait()
-    for d in (1, 2):
-        for a in range(NX):
-            stat_out(d, a).wait_send()
+    for kind in range(2):
+        for d in (1, 2):
+            for a in range(NX):
+                stat_out(kind, d, a).wait_send()
     for copy in ended:
         copy.wait_send()
 
@@ -488,10 +492,10 @@
             pltpu.VMEM((NY, 2, 4, H, 8, HEAD), bf16),
             pltpu.VMEM((4, 2, BLK, HEAD), bf16),
             pltpu.VMEM((NX, TILES, PAIR, PAIR), f32),
-            pltpu.VMEM((2, NX, PAIR, HEAD), f32),
-            pltpu.VMEM((3, NX, 8, PAIR), f32),
+            pltpu.VMEM((NX, PAIR, HEAD), f32),
+            pltpu.VMEM((2, 3, NX, 8, PAIR), f32),
             pltpu.VMEM((3, NX, PAIR, HEAD), bf16),
-            pltpu.VMEM((2, NX, PAIR, HEAD), f32),
+            pltpu.VMEM((NX, 3, PAIR, PAIR), f32),
             dma((11,)),
             dma((4, 8)),
             dma((4, 8)),
@@ -504,8 +508,8 @@
             dma((2, 2, NX)),
             dma((2, 2, UP)),
             dma((2, 2, UP)),
-            dma((2, NX)),
-            dma((2, NX)),
+            dma((2, 2, NX)),
+            dma((2, 2, NX)),
             dma((3, NX, NZ)),
             dma((3, NX, NZ)),
         ],

time: 102 us -> 101 us (level)
  the two profiles are of different devices: /device:TPU:200 before, /device:TPU:64 now
where the time goes in v4:
time: 101 us; the launch traced here: 100 us
  Pallas kernels  99.7 us (99%)
    pallas_call x1, Pallas kernels, backward(): pl.pallas_call(kernel, name='backward', out_shape=(out,) * 3, in_specs=[S...  97.7 us

profile of v4, /device:TPU:64, one launch (start us, length us, event | category | flops | bytes accessed | tf_op | source)
XLA Modules:
  0.0 100.3 jit_solution(7747585075720317499)
XLA Ops:
  0.6 97.7 %backward.1 = (bf16[1,128,1024]{2,1,0:T(8,128)(2,1)}, bf16[1,128,1024]{2,1,0:T(8,128)(2,1)}, bf16[1,128,1024]{2,1,0:T(8,128)(2,1)}) custom-call(s32[8]{0:T(128)} %lengths.1, s32[8]{0:T(128)} %counts.1, s32[4,8]{1,0:T(4,128)} %bitcast.1, s32[64]{0:T(128)} %slots.1, bf16[1,128,1024]{2,1,0:T(8,128)(2,1)} %q_ref.1, bf16[1,128,1024]{2,1,0:T(8,128)(2,1)} %g_ref.1, ...), custom_call_target="tpu_custom_call" | custom-call | tf_op jit(solution)/shard_map/backward/pallas_call | solution.py:475
  98.3 2.0 %finish.1 = (bf16[1,128,1024]{2,1,0:T(8,128)(2,1)}, bf16[1,128,1024]{2,1,0:T(8,128)(2,1)}, bf16[1,128,1024]{2,1,0:T(8,128)(2,1)}) custom-call(bf16[1,128,1024]{2,1,0:T(8,128)(2,1)} %get-tuple-element.6.refs_0_, bf16[1,128,1024]{2,1,0:T(8,128)(2,1)} %get-tuple-element.7.refs_1_, bf16[1,128,1024]{2,1,0:T(8,128)(2,1)} %get-tuple-element.8.refs_2_), custom_call_target="tpu_custom_call" | custom-call | tf_op jit(solution)/shard_map/finish/pallas_call | solution.py:529

commit v5 on v4

--- a/solution.py
+++ b/solution.py
@@ -106,16 +106,19 @@
     return (t - 3) // (BLK // PAIR)
 
 
-def answer(total, g, key_of, value_of, weights):
+def answer(total, g, key_of, value_of, weights, dprobs):
     inverse = 1.0 / total
-    output = jnp.zeros((PAIR, HEAD), jnp.float32)
+    delta = None
     for t in range(TILES):
-        prob = weights[t] * inverse
-        output += dot(prob.astype(jnp.bfloat16), value_of(t))
-    delta = jnp.sum(g.astype(jnp.float32) * output, axis=1, keepdims=True)
+        half = (weights[t] * inverse).astype(jnp.bfloat16)
+        dprob = dot_nt(g, value_of(t))
+        dprobs[t] = dprob
+        part = halves(jnp.add, half.astype(jnp.float32) * dprob)
+        delta = part if delta is None else delta + part
+    delta = jnp.sum(delta, axis=1, keepdims=True)
     grad = jnp.zeros((PAIR, HEAD), jnp.float32)
     for t in range(TILES):
-        ds = (weights[t] * inverse) * (dot_nt(g, value_of(t)) - delta)
+        ds = (weights[t] * inverse) * (dprobs[t] - delta)
         grad += dot(ds.astype(jnp.bfloat16), key_of(t))
     return (grad * (1.0 / math.sqrt(HEAD))).astype(jnp.bfloat16), along_lanes(delta)
 
@@ -136,7 +139,7 @@
 def kernel(
     lengths, counts, lists, slots, q_ref, g_ref, k_ref, v_ref, poolk_ref, poolv_ref,
     gq_out, gk_out, gv_out,
-    pool0, pool1, staged, from_core, staged_z, from_z0, from_z1, picked, kv_ref, qg_ref, pieces, mem_ref, weights, totals, stats, grads, probs,
+    pool0, pool1, staged, from_core, staged_z, from_z0, from_z1, picked, kv_ref, qg_ref, pieces, mem_ref, weights, dprobs, totals, stats, grads, probs,
     own_sem, a2a_send, a2a_recv, core_sems, z_send, z_recv, m_send, m_recv, hop_send, hop_recv, ring_send, ring_recv,
     stat_send, stat_recv, out_send, out_recv,
 ):
@@ -408,7 +411,7 @@
         chunk = chunk_at(a)
         grad, delta = answer(
             totals[chunk][:, :1], cotangent(0, chunk, base_of(chunk)),
-            tile_of(0, chunk), tile_of(1, chunk), weights.at[chunk],
+            tile_of(0, chunk), tile_of(1, chunk), weights.at[chunk], dprobs,
         )
         grads[0, chunk] = grad
         share(1, chunk, a, delta)
@@ -442,10 +445,12 @@
 
     lax.fori_loop(0, 2, weigh_chunk, 0)
     qg.hop(1, 2)
-    lax.fori_loop(2, 4, weigh_chunk, 0)
+    lax.fori_loop(2, 3, weigh_chunk, 0)
     qg.hop(1, 3)
     settle(1)
-    lax.fori_loop(0, 4, answer_chunk, 0)
+    lax.fori_loop(0, 1, answer_chunk, 0)
+    lax.fori_loop(3, 4, weigh_chunk, 0)
+    lax.fori_loop(1, 4, answer_chunk, 0)
     shared(0)
     turned = (y >= NY - 2).astype(jnp.int32)
     for a in range(NX):
@@ -492,6 +497,7 @@
             pltpu.VMEM((NY, 2, 4, H, 8, HEAD), bf16),
             pltpu.VMEM((4, 2, BLK, HEAD), bf16),
             pltpu.VMEM((NX, TILES, PAIR, PAIR), f32),
+            pltpu.VMEM((TILES, PAIR, PAIR), f32),
             pltpu.VMEM((NX, PAIR, HEAD), f32),
             pltpu.VMEM((2, 3, NX, 8, PAIR), f32),
             pltpu.VMEM((3, NX, PAIR, HEAD), bf16),

time: 101 us -> 100 us (0.990)
  the two profiles are of different devices: /device:TPU:64 before, /device:TPU:192 now
where the time goes in v5:
time: 100 us
  Pallas kernels  99.4 us (99%)
    pallas_call x1, Pallas kernels, backward(): pl.pallas_call(kernel, name='backward', out_shape=(out,) * 3, in_specs=[S...  97.4 us
    pallas_call x1, Pallas kernels, finish(): pl.pallas_call(finish_kernel, name='finish', out_shape=tuple((jax.ShapeDt...  2 us

profile of v5, /device:TPU:192, one launch (start us, length us, event | category | flops | bytes accessed | tf_op | source)
XLA Modules:
  0.0 100.1 jit_solution(17528828678595648621)
XLA Ops:
  0.6 97.4 %backward.1 = (bf16[1,128,1024]{2,1,0:T(8,128)(2,1)}, bf16[1,128,1024]{2,1,0:T(8,128)(2,1)}, bf16[1,128,1024]{2,1,0:T(8,128)(2,1)}) custom-call(s32[8]{0:T(128)} %lengths.1, s32[8]{0:T(128)} %counts.1, s32[4,8]{1,0:T(4,128)} %bitcast.1, s32[64]{0:T(128)} %slots.1, bf16[1,128,1024]{2,1,0:T(8,128)(2,1)} %q_ref.1, bf16[1,128,1024]{2,1,0:T(8,128)(2,1)} %g_ref.1, ...), custom_call_target="tpu_custom_call" | custom-call | tf_op jit(solution)/shard_map/backward/pallas_call | solution.py:480
  98.0 2.0 %finish.1 = (bf16[1,128,1024]{2,1,0:T(8,128)(2,1)}, bf16[1,128,1024]{2,1,0:T(8,128)(2,1)}, bf16[1,128,1024]{2,1,0:T(8,128)(2,1)}) custom-call(bf16[1,128,1024]{2,1,0:T(8,128)(2,1)} %get-tuple-element.6.refs_0_, bf16[1,128,1024]{2,1,0:T(8,128)(2,1)} %get-tuple-element.7.refs_1_, bf16[1,128,1024]{2,1,0:T(8,128)(2,1)} %get-tuple-element.8.refs_2_), custom_call_target="tpu_custom_call" | custom-call | tf_op jit(solution)/shard_map/finish/pallas_call | solution.py:535
